TPU v7x, 32 devices: a whole 2x2x4 slice. The times are simulated.
32 devices in a mesh: ctx: 8 (over y, x, core), fsdp: 4 (over z).
Axes of the slice: x: 2, y: 2, z: 4, core: 2. Of those that a mesh axis runs over, the one named last changes fastest.
Arguments:
- tokens: bfloat16 [4, 2048, 2048], P('fsdp', 'ctx'), may hold values from -6 to 6
- cotangent: bfloat16 [4, 2048, 2048], P('fsdp', 'ctx'), may hold values from -6 to 6
- doc_starts: int32 [4, 8], P('fsdp'), may hold values from 0 to 2047, as said below
- deal_order: int32 [16], replicated, may hold values from 0 to 15, as said below
- query_key_value_weight: bfloat16 [2048, 1536], P('fsdp'), may hold values from -0.125 to 0.125
- w_out: bfloat16 [1024, 2048], P('fsdp'), may hold values from -1.5 to 1.5
- w_gate: bfloat16 [2048, 1024], P('fsdp'), may hold values from -0.125 to 0.125
- w_up: bfloat16 [2048, 1024], P('fsdp'), may hold values from -0.125 to 0.125
- w_down: bfloat16 [1024, 2048], P('fsdp'), may hold values from -0.1875 to 0.1875
- gain_attn: bfloat16 [2048], P('fsdp'), may hold values from 0.5 to 1.5
- gain_ffn: bfloat16 [2048], P('fsdp'), may hold values from 0.5 to 1.5
- gain_qk: bfloat16 [2, 64], P(None, 'fsdp'), may hold values from 1 to 2
Outputs:
- mixed_out: bfloat16 [4, 2048, 2048], P('fsdp', 'ctx')
- tokens_grad: float32 [4, 2048, 2048], P('fsdp', 'ctx')
- w_qkv_grad: float32 [2048, 1536], P('fsdp')
- w_out_grad: float32 [1024, 2048], P('fsdp')
- w_gate_grad: float32 [2048, 1024], P('fsdp')
- w_up_grad: float32 [2048, 1024], P('fsdp')
- w_down_grad: float32 [1024, 2048], P('fsdp')
- gain_attn_grad: float32 [2048], P('fsdp')
- gain_ffn_grad: float32 [2048], P('fsdp')
- gain_qk_grad: float32 [2, 64], P(None, 'fsdp')
Inputs may be any that keep to these rules, and one draw needn't show every extreme that they name: `doc_starts`: in each pack the first entry is 0 and entries rise; every document (from its start to the next start, the last one to 2048) holds 1 to 1024 tokens, one document of each pack holds exactly 1024, and the last document of each pack holds one token, so its start is 2047. `deal_order`: A permutation of the 16 blocks of a pack; the blocks at stored places 2 c and 2 c + 1 add up to 15.
All inputs are finite; a program needn't handle non-finite values.
Results may differ from a plain program's by a relative error of at most 0.017.
The roundings to bfloat16 on the way count: a program that leaves them out, or rounds other values in their place, can miss the bound.
Values may be sent and summed in bfloat16 or wider, within the bound.
A program may use at most 192 MiB of HBM per device.

v0:
```python
import math

import jax
import jax.numpy as jnp
from jax import lax
from jax.sharding import PartitionSpec as P

QUERY_HEADS = 16
KEY_VALUE_HEADS = 4
HEAD_SIZE = 64


EPSILON = 1e-06
THETA = 10000.0


def times_transposed(left, right):
    return lax.dot_general(
        left, right, (((1,), (1,)), ((), ())), preferred_element_type=jnp.float32
    )


def transposed_times(left, right):
    return lax.dot_general(
        left, right, (((0,), (0,)), ((), ())), preferred_element_type=jnp.float32
    )


def norm_forward(values, gain_vec):
    inverse = lax.rsqrt(jnp.mean(values * values, axis=-1, keepdims=True) + EPSILON)
    return (values * inverse * gain_vec, inverse)


def norm_backward(values, inverse, gain_vec, grad_out):
    scaled = grad_out * gain_vec
    grad_in = inverse * (
        scaled - values * inverse * inverse * jnp.mean(scaled * values, axis=-1, keepdims=True)
    )
    return (grad_in, grad_out * values * inverse)


def rotate(values, cosines, sine_vals):
    half_dim = values.shape[-1] // 2
    first_half = values[..., :half_dim]
    second_half = values[..., half_dim:]
    return jnp.concatenate(
        [
            first_half * cosines - second_half * sine_vals,
            second_half * cosines + first_half * sine_vals,
        ],
        axis=-1,
    )


def rotate_back(grad_out, cosines, sine_vals):
    half_dim = grad_out.shape[-1] // 2
    first_half = grad_out[..., :half_dim]
    second_half = grad_out[..., half_dim:]
    return jnp.concatenate(
        [
            first_half * cosines + second_half * sine_vals,
            second_half * cosines - first_half * sine_vals,
        ],
        axis=-1,
    )


def rotary_tables(position, doc_begin):
    offsets = (position - doc_begin).astype(jnp.float32)
    frequency = THETA ** (-jnp.arange(0, HEAD_SIZE // 2, dtype=jnp.float32) * 2.0 / HEAD_SIZE)
    angles = offsets[:, None] * frequency[None, :]
    return (jnp.cos(angles)[:, None, :], jnp.sin(angles)[:, None, :])


def per_device(
    tokens,
    cotangent,
    doc_starts,
    deal_order,
    query_key_value_weight,
    w_out,
    w_gate,
    w_up,
    w_down,
    gain_attn,
    gain_ffn,
    gain_qk,
):
    ctx_count = lax.axis_size("ctx")
    fsdp_count = lax.axis_size("fsdp")
    ctx_rank = lax.axis_index("ctx")
    qkv_full, out_full, attn_gathered, qk_gathered = (
        lax.all_gather(query_key_value_weight, "fsdp", axis=0, tiled=True),
        lax.all_gather(w_out, "fsdp", axis=0, tiled=True),
        lax.all_gather(gain_attn, "fsdp", axis=0, tiled=True),
        lax.all_gather(gain_qk, "fsdp", axis=1, tiled=True),
    )
    gate_full, up_full, down_full, ffn_gathered = (
        lax.all_gather(w_gate, "fsdp", axis=0, tiled=True),
        lax.all_gather(w_up, "fsdp", axis=0, tiled=True),
        lax.all_gather(w_down, "fsdp", axis=0, tiled=True),
        lax.all_gather(gain_ffn, "fsdp", axis=0, tiled=True),
    )
    attn_gain = attn_gathered.astype(jnp.float32)
    ffn_gain = ffn_gathered.astype(jnp.float32)
    query_gain = qk_gathered[0].astype(jnp.float32)
    key_gain = qk_gathered[1].astype(jnp.float32)
    pack_in = tokens[0].astype(jnp.float32)
    token_rows = pack_in.shape[0]
    block_len = token_rows // 2
    full_len = token_rows * ctx_count
    key_value_width = KEY_VALUE_HEADS * HEAD_SIZE
    group_width = QUERY_HEADS // KEY_VALUE_HEADS
    inv_root = HEAD_SIZE ** (-0.5)
    start_row = doc_starts[0]
    stored = jnp.arange(full_len, dtype=jnp.int32)
    key_place = (
        jnp.repeat(deal_order, block_len, total_repeat_length=full_len) * block_len
        + stored % block_len
    )
    key_begin = jnp.max(
        jnp.where(start_row[None, :] <= key_place[:, None], start_row[None, :], 0), axis=1
    )
    query_place = lax.dynamic_slice_in_dim(key_place, ctx_rank * token_rows, token_rows)
    query_begin = lax.dynamic_slice_in_dim(key_begin, ctx_rank * token_rows, token_rows)
    cosines, sine_vals = rotary_tables(query_place, query_begin)
    normed, attn_inverse = norm_forward(pack_in, attn_gain)
    normed_low = normed.astype(jnp.bfloat16)
    projected_rows = jnp.dot(normed_low, qkv_full, preferred_element_type=jnp.float32)
    query_raw = projected_rows[:, : QUERY_HEADS * HEAD_SIZE].reshape(
        token_rows, QUERY_HEADS, HEAD_SIZE
    )
    unrotated_key = projected_rows[
        :, QUERY_HEADS * HEAD_SIZE : (QUERY_HEADS + KEY_VALUE_HEADS) * HEAD_SIZE
    ].reshape(token_rows, KEY_VALUE_HEADS, HEAD_SIZE)
    unprojected_value = projected_rows[:, (QUERY_HEADS + KEY_VALUE_HEADS) * HEAD_SIZE :]
    query_normed, query_inverse = norm_forward(query_raw, query_gain)
    key_normed, key_inverse = norm_forward(unrotated_key, key_gain)
    query_heads_rows = rotate(query_normed, cosines, sine_vals).astype(jnp.bfloat16)
    key_local = rotate(key_normed, cosines, sine_vals).astype(jnp.bfloat16)
    local_pair = jnp.concatenate(
        [key_local.reshape(token_rows, key_value_width), unprojected_value.astype(jnp.bfloat16)],
        axis=1,
    )
    every_pair = lax.all_gather(local_pair, "ctx", axis=0, tiled=True)
    key_block_index = math.gcd(full_len, 512)
    block_total = full_len // key_block_index
    key_block_list = (
        every_pair[:, :key_value_width].reshape(
            block_total, key_block_index, KEY_VALUE_HEADS, HEAD_SIZE
        ),
        key_place.reshape(block_total, key_block_index),
        key_begin.reshape(block_total, key_block_index),
        every_pair[:, key_value_width:].reshape(
            block_total, key_block_index, KEY_VALUE_HEADS, HEAD_SIZE
        ),
    )
    grouped_heads = query_heads_rows.reshape(token_rows, KEY_VALUE_HEADS, group_width, HEAD_SIZE)

    def block_scores(key_tile, place_tile, begin_tile):
        raw_scores = (
            jnp.einsum(
                "qkgd,tkd->kgqt", grouped_heads, key_tile, preferred_element_type=jnp.float32
            )
            * inv_root
        )
        allowed = (query_begin[:, None] == begin_tile[None, :]) & (
            place_tile[None, :] <= query_place[:, None]
        )
        return jnp.where(allowed[None, None], raw_scores, -1e30)

    def stats_step(carry, tiles):
        row_max, row_sum = carry
        scores = block_scores(tiles[0], tiles[1], tiles[2])
        new_max = jnp.maximum(row_max, jnp.max(scores, axis=-1))
        row_sum = row_sum * jnp.exp(row_max - new_max) + jnp.sum(
            jnp.exp(scores - new_max[..., None]), axis=-1
        )
        return ((new_max, row_sum), None)

    initial_maximum = jnp.full((KEY_VALUE_HEADS, group_width, token_rows), -1e30, jnp.float32)
    initial_sum = jnp.zeros((KEY_VALUE_HEADS, group_width, token_rows), jnp.float32)
    (row_max, row_sum), unused = lax.scan(
        stats_step, (initial_maximum, initial_sum), key_block_list
    )

    def block_probs(tiles):
        scores = block_scores(tiles[0], tiles[1], tiles[2])
        return jnp.exp(scores - row_max[..., None]) / row_sum[..., None]

    def output_update(running, tiles):
        soft_probs = block_probs(tiles).astype(jnp.bfloat16)
        return (
            running
            + jnp.einsum(
                "kgqt,tkd->qkgd", soft_probs, tiles[3], preferred_element_type=jnp.float32
            ),
            None,
        )

    attended_sum, unused = lax.scan(
        output_update,
        jnp.zeros((token_rows, KEY_VALUE_HEADS, group_width, HEAD_SIZE), jnp.float32),
        key_block_list,
    )
    attended = attended_sum.reshape(token_rows, QUERY_HEADS * HEAD_SIZE).astype(jnp.bfloat16)
    hidden_in = pack_in + jnp.dot(attended, out_full, preferred_element_type=jnp.float32)
    normed_ffn, ffn_inverse = norm_forward(hidden_in, ffn_gain)
    normed_ffn_low = normed_ffn.astype(jnp.bfloat16)
    gate_act = jnp.dot(normed_ffn_low, gate_full, preferred_element_type=jnp.float32)
    upward = jnp.dot(normed_ffn_low, up_full, preferred_element_type=jnp.float32)
    sigmoid_gate = jax.nn.sigmoid(gate_act)
    hidden = (gate_act * sigmoid_gate * upward).astype(jnp.bfloat16)
    mixed_out = (hidden_in + jnp.dot(hidden, down_full, preferred_element_type=jnp.float32)).astype(
        jnp.bfloat16
    )
    grad_mixed = cotangent[0]
    grad_hidden = times_transposed(grad_mixed, down_full)
    grad_gate = (
        grad_hidden * upward * sigmoid_gate * (1.0 + gate_act * (1.0 - sigmoid_gate))
    ).astype(jnp.bfloat16)
    grad_up = (grad_hidden * gate_act * sigmoid_gate).astype(jnp.bfloat16)
    grad_normed_ffn = times_transposed(grad_gate, gate_full) + times_transposed(grad_up, up_full)
    grad_resid_part, ffn_gain_part = norm_backward(
        hidden_in, ffn_inverse, ffn_gain, grad_normed_ffn
    )
    grad_resid = grad_mixed.astype(jnp.float32) + grad_resid_part
    grad_branch = grad_resid.astype(jnp.bfloat16)
    attended_gradient = times_transposed(grad_branch, out_full).astype(jnp.bfloat16)
    grouped_gradient = attended_gradient.reshape(
        token_rows, KEY_VALUE_HEADS, group_width, HEAD_SIZE
    )

    def delta_update(running, tiles):
        soft_probs = block_probs(tiles)
        grad_probs = jnp.einsum(
            "qkgd,tkd->kgqt", grouped_gradient, tiles[3], preferred_element_type=jnp.float32
        )
        return (running + jnp.sum(soft_probs * grad_probs, axis=-1), None)

    row_delta, unused = lax.scan(
        delta_update,
        jnp.zeros((KEY_VALUE_HEADS, group_width, token_rows), jnp.float32),
        key_block_list,
    )

    def gradient_update(running, tiles):
        soft_probs = block_probs(tiles)
        grad_probs = jnp.einsum(
            "qkgd,tkd->kgqt", grouped_gradient, tiles[3], preferred_element_type=jnp.float32
        )
        grad_scores = (soft_probs * (grad_probs - row_delta[..., None])).astype(jnp.bfloat16)
        running = running + jnp.einsum(
            "kgqt,tkd->qkgd", grad_scores, tiles[0], preferred_element_type=jnp.float32
        )
        grad_keys = (
            jnp.einsum(
                "kgqt,qkgd->tkd", grad_scores, grouped_heads, preferred_element_type=jnp.float32
            )
            * inv_root
        )
        grad_values = jnp.einsum(
            "kgqt,qkgd->tkd",
            soft_probs.astype(jnp.bfloat16),
            grouped_gradient,
            preferred_element_type=jnp.float32,
        )
        return (
            running,
            jnp.concatenate(
                [
                    grad_keys.reshape(key_block_index, key_value_width),
                    grad_values.reshape(key_block_index, key_value_width),
                ],
                axis=1,
            ),
        )

    query_running, pair_grads = lax.scan(
        gradient_update,
        jnp.zeros((token_rows, KEY_VALUE_HEADS, group_width, HEAD_SIZE), jnp.float32),
        key_block_list,
    )
    grad_query_rot = query_running.reshape(token_rows, QUERY_HEADS, HEAD_SIZE) * inv_root
    local_gradients = lax.psum_scatter(
        pair_grads.reshape(full_len, 2 * key_value_width).astype(jnp.bfloat16),
        "ctx",
        scatter_dimension=0,
        tiled=True,
    ).astype(jnp.float32)
    rotated_key_gradient = local_gradients[:, :key_value_width].reshape(
        token_rows, KEY_VALUE_HEADS, HEAD_SIZE
    )
    grad_value = local_gradients[:, key_value_width:]
    grad_query, query_gain_part = norm_backward(
        query_raw, query_inverse, query_gain, rotate_back(grad_query_rot, cosines, sine_vals)
    )
    grad_key, key_gain_part = norm_backward(
        unrotated_key, key_inverse, key_gain, rotate_back(rotated_key_gradient, cosines, sine_vals)
    )
    grad_projected = jnp.concatenate(
        [
            grad_query.reshape(token_rows, QUERY_HEADS * HEAD_SIZE),
            grad_key.reshape(token_rows, key_value_width),
            grad_value,
        ],
        axis=1,
    ).astype(jnp.bfloat16)
    grad_normed = times_transposed(grad_projected, qkv_full)
    grad_input_part, attn_gain_part = norm_backward(pack_in, attn_inverse, attn_gain, grad_normed)
    tokens_grad = grad_resid + grad_input_part

    def arrange(values):
        leading = values.shape[:-1]
        last_len = values.shape[-1]
        split_view = values.reshape(
            leading + (fsdp_count, ctx_count, last_len // (fsdp_count * ctx_count))
        )
        return jnp.swapaxes(split_view, -3, -2).reshape(leading + (last_len,))

    qk_sum = jnp.stack([jnp.sum(query_gain_part, axis=(0, 1)), jnp.sum(key_gain_part, axis=(0, 1))])
    qk_major = jnp.transpose(
        qk_sum.reshape(2, fsdp_count, HEAD_SIZE // fsdp_count), (1, 0, 2)
    ).reshape(2 * HEAD_SIZE)
    grad_qkv = transposed_times(arrange(normed_low), grad_projected)
    grad_out = transposed_times(arrange(attended), grad_branch)
    grad_wgate = transposed_times(arrange(normed_ffn_low), grad_gate)
    grad_wup = transposed_times(arrange(normed_ffn_low), grad_up)
    grad_wdown = transposed_times(arrange(hidden), grad_mixed)
    grad_attn_gain = arrange(jnp.sum(attn_gain_part, axis=0))
    grad_ffn_gain = arrange(jnp.sum(ffn_gain_part, axis=0))
    grad_qk_gain = arrange(qk_major)
    pieces = (
        lax.psum_scatter(grad_qkv, ("ctx", "fsdp"), scatter_dimension=0, tiled=True),
        lax.psum_scatter(grad_out, ("ctx", "fsdp"), scatter_dimension=0, tiled=True),
        lax.psum_scatter(grad_wgate, ("ctx", "fsdp"), scatter_dimension=0, tiled=True),
        lax.psum_scatter(grad_wup, ("ctx", "fsdp"), scatter_dimension=0, tiled=True),
        lax.psum_scatter(grad_wdown, ("ctx", "fsdp"), scatter_dimension=0, tiled=True),
        lax.psum_scatter(grad_attn_gain, ("ctx", "fsdp"), scatter_dimension=0, tiled=True),
        lax.psum_scatter(grad_ffn_gain, ("ctx", "fsdp"), scatter_dimension=0, tiled=True),
        lax.psum_scatter(grad_qk_gain, ("ctx", "fsdp"), scatter_dimension=0, tiled=True),
    )
    totals = (
        lax.all_gather(pieces[0].astype(jnp.bfloat16), "ctx", axis=0, tiled=True).astype(
            jnp.float32
        ),
        lax.all_gather(pieces[1].astype(jnp.bfloat16), "ctx", axis=0, tiled=True).astype(
            jnp.float32
        ),
        lax.all_gather(pieces[2].astype(jnp.bfloat16), "ctx", axis=0, tiled=True).astype(
            jnp.float32
        ),
        lax.all_gather(pieces[3].astype(jnp.bfloat16), "ctx", axis=0, tiled=True).astype(
            jnp.float32
        ),
        lax.all_gather(pieces[4].astype(jnp.bfloat16), "ctx", axis=0, tiled=True).astype(
            jnp.float32
        ),
        lax.all_gather(pieces[5].astype(jnp.bfloat16), "ctx", axis=0, tiled=True).astype(
            jnp.float32
        ),
        lax.all_gather(pieces[6].astype(jnp.bfloat16), "ctx", axis=0, tiled=True).astype(
            jnp.float32
        ),
        lax.all_gather(pieces[7].astype(jnp.bfloat16), "ctx", axis=0, tiled=True).astype(
            jnp.float32
        ),
    )
    qk_shard = totals[7].reshape(2, HEAD_SIZE // fsdp_count)
    return (
        mixed_out[None],
        tokens_grad[None],
        totals[0],
        totals[1],
        totals[2],
        totals[3],
        totals[4],
        totals[5],
        totals[6],
        qk_shard,
    )


def solution(mesh):
    return jax.shard_map(
        per_device,
        mesh=mesh,
        in_specs=(
            P("fsdp", "ctx", None),
            P("fsdp", "ctx", None),
            P("fsdp", None),
            P(),
            P("fsdp", None),
            P("fsdp", None),
            P("fsdp", None),
            P("fsdp", None),
            P("fsdp", None),
            P("fsdp"),
            P("fsdp"),
            P(None, "fsdp"),
        ),
        out_specs=(
            P("fsdp", "ctx", None),
            P("fsdp", "ctx", None),
            P("fsdp", None),
            P("fsdp", None),
            P("fsdp", None),
            P("fsdp", None),
            P("fsdp", None),
            P("fsdp"),
            P("fsdp"),
            P(None, "fsdp"),
        ),
        check_vma=False,
    )
```

profile of v0, /device:TPU:1, one launch (start us, length us, event | category | flops | bytes accessed | tf_op | source)
XLA Modules:
  0.0 1678.2 jit_solution(975257978420920304)
XLA Ops:
  8.7 10.4 all-gather
  19.7 8.4 all-gather.1
  30.1 4.3 compare_select_fusion.1
  34.7 5.8 fusion.96
  41.9 85.3 %all-gather.15.cloned.1.call-done = bf16[2048,1536]{1,0:T(8,128)(2,1)} async-done(((bf16[512,1536]{1,0:T(8,128)(2,1)}), bf16[2048,1536]{1,0:T(8,128)(2,1)}) %all-gather.15.cloned.1.call-update) | async-done | bytes 6291472 | tf_op jit(solution)/shard_map/all_gather | solution.py:93
  127.2 4.6 fusion.79
  136.5 9.6 all-gather.2
  149.8 10.3 all-gather.17.cloned.1.call-done
  171.4 40.3 %while.49 = (s32[]{:T(128)}, f32[4,4,256]{2,1,0:T(4,128)S(1)}, f32[4,4,256]{2,1,0:T(4,128)S(1)}, s32[256]{0:T(256)S(1)}, s32[4,512]{1,0:T(4,128)S(1)}, /*index=5...) while((s32[]{:T(128)}, f32[4,4,256]{2,1,0:T(4,128)S(1)}, ...), condition=%wide.region_7.8_spmd.clone, body=%wide.region_4.7_spmd.clone.sunk | while | flops 283529216 | bytes 18184328 | solution.py:183
  171.6 4.6 fusion.177
  176.2 5.1 exponential_reduce_fusion.2
  181.7 4.6 fusion.177
  186.3 5.2 exponential_reduce_fusion.2
  191.8 4.6 fusion.177
  196.4 5.2 exponential_reduce_fusion.2
  201.9 4.6 fusion.177
  206.5 5.1 exponential_reduce_fusion.2
  211.7 20.6 %while.50 = (s32[]{:T(128)}, f32[256,4,4,64]{0,3,2,1:T(8,128)}, bf16[4,512,4,64]{1,3,2,0:T(8,128)(2,1)S(1)}, s32[256]{0:T(256)S(1)}, s32[4,512]{1,0:T(4,128)S(1)...) while((s32[]{:T(128)}, f32[256,4,4,64]{0,3,2,1:T(8,128)}, ...), condition=%wide.region_9.10_spmd.clone, body=%wide.region_8.9_spmd.clone.sunk | while | flops 548274176 | bytes 3456658 | solution.py:201
  211.9 3.9 fusion.183
  216.1 5.2 fusion.183
  221.5 5.2 fusion.183
  226.9 5.2 fusion.183
  234.3 7.6 all-gather.19.cloned.1.call-done
  242.0 3.9 multiply_reduce_fusion.2
  247.3 75.3 %all-gather.21.cloned.1.call-done = bf16[2048,1024]{1,0:T(8,128)(2,1)} async-done(((bf16[512,1024]{1,0:T(8,128)(2,1)}), bf16[2048,1024]{1,0:T(8,128)(2,1)}) %all-gather.21.cloned.1.call-update) | async-done | bytes 4194320 | tf_op jit(solution)/shard_map/all_gather | solution.py:99
  322.6 4.7 fusion.108
  327.4 75.9 %all-gather.23.cloned.1.call-done = bf16[2048,1024]{1,0:T(8,128)(2,1)} async-done(((bf16[512,1024]{1,0:T(8,128)(2,1)}), bf16[2048,1024]{1,0:T(8,128)(2,1)}) %all-gather.23.cloned.1.call-update) | async-done | bytes 4194320 | tf_op jit(solution)/shard_map/all_gather | solution.py:100
  403.3 4.7 fusion.109
  408.0 75.9 %all-gather.25.cloned.1.call-done = bf16[1024,2048]{1,0:T(8,128)(2,1)} async-done(((bf16[256,2048]{1,0:T(8,128)(2,1)}), bf16[1024,2048]{1,0:T(8,128)(2,1)}) %all-gather.25.cloned.1.call-update) | async-done | bytes 4194320 | tf_op jit(solution)/shard_map/all_gather | solution.py:101
  484.0 5.7 multiply_convert_fusion.2
  499.2 22.9 %while.51 = (s32[]{:T(128)}, f32[4,4,256]{2,1,0:T(4,128)S(1)}, s32[256]{0:T(256)S(1)}, s32[4,512]{1,0:T(4,128)S(1)}, s32[4,512]{1,0:T(4,128)S(1)}, /*index=5*/s3...) while((s32[]{:T(128)}, f32[4,4,256]{2,1,0:T(4,128)S(1)}, ...), condition=%wide.region_14.15_spmd.clone, body=%wide.region_12.14_spmd.clone.sunk | while | flops 549851136 | bytes 18725024 | solution.py:241
  502.1 3.1 fusion.189
  507.7 3.1 fusion.189
  513.3 3.1 fusion.189
  519.0 3.1 fusion.189
  522.1 69.2 %while.52 = (s32[]{:T(128)}, f32[256,4,4,64]{0,3,2,1:T(8,128)S(1)}, bf16[4,512,512]{1,2,0:T(8,128)(2,1)}, bf16[4,512,4,64]{1,3,2,0:T(8,128)(2,1)S(1)}, s32[256]{...) while((s32[]{:T(128)}, f32[256,4,4,64]{0,3,2,1:T(8,128)S(1)}, ...), condition=%wide.region_16.17_spmd.clone, body=%wide.region_15.16_spmd.clone.sunk | while | flops 1361182720 | bytes 94959864 | solution.py:279
  524.7 4.5 fusion.201
  532.3 4.9 fusion.203
  542.0 4.5 fusion.201
  549.6 4.9 fusion.203
  559.3 4.5 fusion.201
  566.9 4.9 fusion.203
  576.6 4.5 fusion.201
  584.2 4.9 fusion.203
  591.3 4.1 copy.197
  596.6 6.2 fusion.87
  606.7 4.5 fusion.111
  612.2 4.5 fusion.112
  618.1 4.5 fusion.81
  640.2 3.2 multiply_reduce_fusion.3
  649.1 7.7 fusion.90
  656.9 165.4 %reduce-scatter.11.cloned.1.call-done = f32[32,2048]{1,0:T(8,128)} async-done(((f32[1024,2048]{1,0:T(8,128)}), f32[32,2048]{1,0:T(8,128)}) %reduce-scatter.11.cloned.1.call-update) | async-done | bytes 262160 | tf_op jit(solution)/shard_map/reduce_scatter | solution.py:335
  824.0 184.0 %reduce-scatter.13.cloned.1.call-done = f32[64,1024]{1,0:T(8,128)} async-done(((f32[2048,1024]{1,0:T(8,128)}), f32[64,1024]{1,0:T(8,128)}) %reduce-scatter.13.cloned.1.call-update) | async-done | bytes 262160 | tf_op jit(solution)/shard_map/reduce_scatter | solution.py:336
  1009.7 183.9 %reduce-scatter.15.cloned.1.call-done = f32[64,1024]{1,0:T(8,128)} async-done(((f32[2048,1024]{1,0:T(8,128)}), f32[64,1024]{1,0:T(8,128)}) %reduce-scatter.15.cloned.1.call-update) | async-done | bytes 262160 | tf_op jit(solution)/shard_map/reduce_scatter | solution.py:337
  1195.3 184.1 %reduce-scatter.17.cloned.1.call-done = f32[32,2048]{1,0:T(8,128)} async-done(((f32[1024,2048]{1,0:T(8,128)}), f32[32,2048]{1,0:T(8,128)}) %reduce-scatter.17.cloned.1.call-update) | async-done | bytes 262160 | tf_op jit(solution)/shard_map/reduce_scatter | solution.py:338
  1381.0 155.9 %reduce-scatter.9.cloned.1.call-done = f32[64,1536]{1,0:T(8,128)} async-done(((f32[2048,1536]{1,0:T(8,128)}), f32[64,1536]{1,0:T(8,128)}) %reduce-scatter.9.cloned.1.call-update) | async-done | bytes 393232 | tf_op jit(solution)/shard_map/reduce_scatter | solution.py:334
  1540.9 4.6 fusion.61
  1545.6 6.3 fusion.73
  1552.4 41.3 %all-reduce.6 = (bf16[2048]{0:T(1024)(128)(2,1)S(1)}, bf16[2048]{0:T(1024)(128)(2,1)S(1)}, bf16[128]{0:T(256)(128)(2,1)S(1)}) all-reduce(f32[2048]{0:T(1024)S(1)} %reshape.630, f32[2048]{0:T(1024)S(1)} %reshape.632, f32[128]{0:T(128)S(1)} %reshape.633), channel_id=8, replica_groups=mesh['ctx'=8,'fsdp'=4] {'ctx','fsdp'}, use_global_device_ids=true, to_apply=%region_27.28.clone | all-reduce | flops 4224 | bytes 25344
  1594.6 12.6 all-reduce.7
  1609.0 3.5 fusion.69
  1620.9 19.1 %all-gather.35.cloned.1.call-done = bf16[256,2048]{1,0:T(8,128)(2,1)} async-done(((bf16[32,2048]{1,0:T(8,128)(2,1)}), bf16[256,2048]{1,0:T(8,128)(2,1)}) %all-gather.35.cloned.1.call-update) | async-done | bytes 1048592 | tf_op jit(solution)/shard_map/all_gather | solution.py:356
  1642.8 25.1 %all-gather.27.cloned.1.call-done = bf16[512,1536]{1,0:T(8,128)(2,1)} async-done(((bf16[64,1536]{1,0:T(8,128)(2,1)}), bf16[512,1536]{1,0:T(8,128)(2,1)}) %all-gather.27.cloned.1.call-update) | async-done | bytes 1572880 | tf_op jit(solution)/shard_map/all_gather | solution.py:344
  1667.9 3.5 convert_element_type.179
  (368 shorter events, 135.1 us)
Async XLA Ops:
  7.2 34.2 %copy-start.7 = (bf16[1,256,2048]{2,1,0:T(8,128)(2,1)S(1)}, bf16[1,256,2048]{2,1,0:T(8,128)(2,1)}, u32[]{:S(2)}) copy-start(bf16[1,256,2048]{2,1,0:T(8,128)(2,1)} %param.22) | copy-start | bytes 3145732
  7.2 120.0 %all-gather.15.cloned.1.call-start = ((), (), s32[]{:S(2)}) async-start(), calls=%async_computation.6 | async-start | bytes 7864320 | tf_op jit(solution)/shard_map/all_gather | solution.py:93
  7.9 152.2 %all-gather.17.cloned.1.call-start = ((), (), s32[]{:S(2)}) async-start(), calls=%async_computation.7 | async-start | bytes 2359296 | tf_op jit(solution)/shard_map/all_gather | solution.py:145
  19.6 112.2 %copy-start.46 = (f32[4,1,512]{2,1,0:T(1,128)}, f32[4,1,512]{2,1,0:T(1,128)S(1)}, u32[]{:S(2)}) copy-start(f32[4,1,512]{2,1,0:T(1,128)S(1)} %convert_element_type.198) | copy-start | bytes 24580
  41.6 90.5 %copy-start.50 = (f32[64]{0:T(128)}, f32[64]{0:T(128)S(1)}, u32[]{:S(2)}) copy-start(f32[64]{0:T(128)S(1)} %get-tuple-element.802) | copy-start | bytes 772
  41.6 107.3 %copy-start.52 = (f32[64]{0:T(128)}, f32[64]{0:T(128)S(1)}, u32[]{:S(2)}) copy-start(f32[64]{0:T(128)S(1)} %get-tuple-element.801) | copy-start | bytes 772
  41.7 90.2 %copy-start.48 = (f32[256]{0:T(256)}, f32[256]{0:T(256)S(1)}, u32[]{:S(2)}) copy-start(f32[256]{0:T(256)S(1)} %add_rsqrt_fusion.3) | copy-start | bytes 3076
  41.9 107.3 %copy-start.29 = (f32[256,32]{0,1:T(8,128)}, f32[256,32]{0,1:T(8,128)S(1)}, u32[]{:S(2)}) copy-start(f32[256,32]{0,1:T(8,128)S(1)} %get-tuple-element.799) | copy-start | bytes 98308
  41.9 107.3 %copy-start.31 = (f32[256,32]{0,1:T(8,128)}, f32[256,32]{0,1:T(8,128)S(1)}, u32[]{:S(2)}) copy-start(f32[256,32]{0,1:T(8,128)S(1)} %get-tuple-element.800) | copy-start | bytes 98308
  131.8 14.3 copy-start.17
  132.0 3.1 copy-start.23
  133.8 2.7 copy-start.56
  133.8 12.2 copy-start.54
  133.8 12.2 copy-start.55
  133.8 108.1 %all-gather.19.cloned.1.call-start = ((), (), s32[]{:S(2)}) async-start(), calls=%async_computation.8 | async-start | bytes 5242880 | tf_op jit(solution)/shard_map/all_gather | solution.py:94
  134.6 188.1 %all-gather.21.cloned.1.call-start = ((), (), s32[]{:S(2)}) async-start(), calls=%async_computation.9 | async-start | bytes 5242880 | tf_op jit(solution)/shard_map/all_gather | solution.py:99
  135.2 268.1 %all-gather.23.cloned.1.call-start = ((), (), s32[]{:S(2)}) async-start(), calls=%async_computation.10 | async-start | bytes 5242880 | tf_op jit(solution)/shard_map/all_gather | solution.py:100
  135.8 348.2 %all-gather.25.cloned.1.call-start = ((), (), s32[]{:S(2)}) async-start(), calls=%async_computation.11 | async-start | bytes 5242880 | tf_op jit(solution)/shard_map/all_gather | solution.py:101
  136.3 507.1 %reduce-scatter.7.cloned.1.call-start = ((), (), s32[]{:S(2)}) async-start(), calls=%async_computation.12 | async-start | bytes 2359296 | tf_op jit(solution)/shard_map/reduce_scatter | solution.py:285
  232.3 9.7 copy-start.11
  232.3 9.7 copy-start.14
  234.3 11.5 copy-start.15
  245.8 248.9 %copy-start.3 = (f32[256,2048]{1,0:T(8,128)}, f32[256,2048]{1,0:T(8,128)S(1)}, u32[]{:S(2)}) copy-start(f32[256,2048]{1,0:T(8,128)S(1)} %get-tuple-element.820) | copy-start | bytes 6291460
  484.0 5.7 copy-start.57
  494.7 2.9 copy-start.13
  499.2 22.9 %copy-start.2 = (f32[256,4,4,64]{0,3,2,1:T(8,128)S(1)}, f32[256,4,4,64]{0,3,2,1:T(8,128)}, u32[]{:S(2)}) copy-start(f32[256,4,4,64]{0,3,2,1:T(8,128)} %custom-call.4) | copy-start | bytes 3145732
  524.7 4.5 copy-start.1
  532.3 4.9 copy-start
  542.0 4.5 copy-start.1
  549.6 4.9 copy-start
  559.3 4.5 copy-start.1
  566.9 4.9 copy-start
  576.6 4.5 copy-start.1
  584.2 4.9 copy-start
  595.5 226.8 %reduce-scatter.11.cloned.1.call-start = ((), (), s32[]{:S(2)}) async-start(), calls=%async_computation.15 | async-start | bytes 8650752 | tf_op jit(solution)/shard_map/reduce_scatter | solution.py:335
  602.8 3.9 copy-start.37
  602.8 405.3 %reduce-scatter.13.cloned.1.call-start = ((), (), s32[]{:S(2)}) async-start(), calls=%async_computation.17 | async-start | bytes 8650752 | tf_op jit(solution)/shard_map/reduce_scatter | solution.py:336
  611.2 582.4 %reduce-scatter.15.cloned.1.call-start = ((), (), s32[]{:S(2)}) async-start(), calls=%async_computation.19 | async-start | bytes 8650752 | tf_op jit(solution)/shard_map/reduce_scatter | solution.py:337
  616.8 762.6 %reduce-scatter.17.cloned.1.call-start = ((), (), s32[]{:S(2)}) async-start(), calls=%async_computation.21 | async-start | bytes 8650752 | tf_op jit(solution)/shard_map/reduce_scatter | solution.py:338
  622.6 2.8 copy-start.51
  622.6 3.4 copy-start.53
  622.6 3.5 copy-start.42
  622.7 3.6 copy-start.49
  622.7 914.3 %reduce-scatter.9.cloned.1.call-start = ((), (), s32[]{:S(2)}) async-start(), calls=%async_computation.13 | async-start | bytes 12976128 | tf_op jit(solution)/shard_map/reduce_scatter | solution.py:334
  626.3 3.0 copy-start.44
  631.2 2.7 copy-start.30
  631.2 2.7 copy-start.32
  636.6 3.6 copy-start.18
  640.2 5.1 copy-start.24
  645.2 2.8 copy-start.28
  645.3 3.8 copy-start.33
  649.0 7.7 copy-start.34
  656.8 881.8 %copy-start.58 = (u32[32]{0:T(128)S(1)}, u32[32]{0:T(128)}, u32[]{:S(2)}) copy-start(u32[32]{0:T(128)} %constant.241) | copy-start | bytes 388
  656.8 883.7 %copy-start.45 = (f32[2048]{0:T(1024)S(1)}, f32[2048]{0:T(1024)}, u32[]{:S(2)}) copy-start(f32[2048]{0:T(1024)} %get-tuple-element.648) | copy-start | bytes 24580
  656.8 884.0 %copy-start.4 = (f32[256,2048]{1,0:T(8,128)S(1)}, f32[256,2048]{1,0:T(8,128)}, u32[]{:S(2)}) copy-start(f32[256,2048]{1,0:T(8,128)} %copy-done.3) | copy-start | bytes 6291460
  656.9 955.7 %all-gather.29.cloned.1.call-start = ((), (), s32[]{:S(2)}) async-start(), calls=%async_computation.16 | async-start | bytes 1179648 | tf_op jit(solution)/shard_map/all_gather | solution.py:347
  824.0 791.3 %all-gather.31.cloned.1.call-start = ((), (), s32[]{:S(2)}) async-start(), calls=%async_computation.18 | async-start | bytes 1179648 | tf_op jit(solution)/shard_map/all_gather | solution.py:350
  1009.7 608.4 %all-gather.33.cloned.1.call-start = ((), (), s32[]{:S(2)}) async-start(), calls=%async_computation.20 | async-start | bytes 1179648 | tf_op jit(solution)/shard_map/all_gather | solution.py:353
  1195.2 444.8 %all-gather.35.cloned.1.call-start = ((), (), s32[]{:S(2)}) async-start(), calls=%async_computation.22 | async-start | bytes 1179648 | tf_op jit(solution)/shard_map/all_gather | solution.py:356
  1381.0 287.0 %all-gather.27.cloned.1.call-start = ((), (), s32[]{:S(2)}) async-start(), calls=%async_computation.14 | async-start | bytes 1769472 | tf_op jit(solution)/shard_map/all_gather | solution.py:344
  1540.9 4.7 copy-start.25
  1540.9 4.7 copy-start.35
  1540.9 4.7 copy-start.47
  1545.6 63.4 %copy-start.6 = (f32[256,2048]{1,0:T(8,128)S(1)}, f32[256,2048]{1,0:T(8,128)}, u32[]{:S(2)}) copy-start(f32[256,2048]{1,0:T(8,128)} %copy-done.5) | copy-start | bytes 6291460
  (18 other events, 23.9 us)
Sparse Core Ops, SparseCore 0:
  9.6 117.5 all-gather.14
  133.9 26.1 all-gather.16
  161.7 80.1 all-gather.18
  243.4 79.2 all-gather.20
  324.1 79.2 all-gather.22
  404.7 79.2 all-gather.24
  595.6 39.5 reduce-scatter.6
  637.5 184.7 reduce-scatter.10
  824.6 183.3 reduce-scatter.12
  1010.2 183.3 reduce-scatter.14
  1195.9 183.3 reduce-scatter.16
  1385.2 151.6 reduce-scatter.8
  1539.4 25.1 all-gather.28
  1566.4 23.2 all-gather.30
  1591.4 23.4 all-gather.32
  1616.6 23.3 all-gather.34
  1642.3 25.5 all-gather.26
where the time goes:
time: 1680 us
  waiting for transfers between devices  1250 us (74%)
  matrix products  191 us (11%)
  blocking collectives  82.3 us (5%)
  other arithmetic  81.5 us (5%)
  local copies, waits for them, and re-layouts  53.6 us (3%)
    reduce_scatter x1, waiting for transfers between devices, per_device(): lax.psum_scatter(grad_wdown, ('ctx', 'fsdp'), scatter_dimension=0, tiled=...  184 us
    reduce_scatter x1, waiting for transfers between devices, per_device(): lax.psum_scatter(grad_wgate, ('ctx', 'fsdp'), scatter_dimension=0, tiled=...  184 us
    reduce_scatter x1, waiting for transfers between devices, per_device(): lax.psum_scatter(grad_wup, ('ctx', 'fsdp'), scatter_dimension=0, tiled=True)  184 us
    reduce_scatter x1, waiting for transfers between devices, per_device(): lax.psum_scatter(grad_out, ('ctx', 'fsdp'), scatter_dimension=0, tiled=True)  165 us
    reduce_scatter x1, waiting for transfers between devices, per_device(): lax.psum_scatter(grad_qkv, ('ctx', 'fsdp'), scatter_dimension=0, tiled=True)  156 us
    all_gather x1, waiting for transfers between devices, per_device(): lax.all_gather(query_key_value_weight, 'fsdp', axis=0, tiled=True)  85.3 us
    all_gather x1, waiting for transfers between devices, per_device(): lax.all_gather(w_down, 'fsdp', axis=0, tiled=True)  75.9 us
    all_gather x1, waiting for transfers between devices, per_device(): lax.all_gather(w_up, 'fsdp', axis=0, tiled=True)  75.9 us
  transfers between devices with their start and end apart: 17, of which 13 were waited for; matrix products, arithmetic and copies ran while one was open for 12% of the time, Pallas kernels for 0%

commit v1 on v0

--- a/solution.py
+++ b/solution.py
@@ -1,8 +1,11 @@
+import functools
 import math
 
 import jax
 import jax.numpy as jnp
 from jax import lax
+from jax.experimental import pallas as pl
+from jax.experimental.pallas import tpu as pltpu
 from jax.sharding import PartitionSpec as P
 
 QUERY_HEADS = 16
@@ -70,6 +73,616 @@
     frequency = THETA ** (-jnp.arange(0, HEAD_SIZE // 2, dtype=jnp.float32) * 2.0 / HEAD_SIZE)
     angles = offsets[:, None] * frequency[None, :]
     return (jnp.cos(angles)[:, None, :], jnp.sin(angles)[:, None, :])
+
+
+MESH = pl.DeviceIdType.MESH
+DMA = pltpu.SemaphoreType.DMA
+HBM_SPEC = pl.BlockSpec(memory_space=pl.ANY)
+SPACING = 2
+
+
+def plane_shape(ctx_count):
+    chips = ctx_count // 2
+    bits = chips.bit_length() - 1
+    assert 2**bits == chips and ctx_count == 2 * chips
+    return chips, bits
+
+
+class Place:
+    def __init__(self, ctx_count, fsdp_count):
+        self.chips, self.bits = plane_shape(ctx_count)
+        self.fsdp_count = fsdp_count
+        self.ctx = lax.axis_index("ctx")
+        self.z = lax.axis_index("fsdp")
+        self.core = self.ctx % 2
+        chip = self.ctx // 2
+        self.bit = [(chip // 2**j) % 2 for j in range(self.bits)]
+        self.across = [self.ctx + (1 - 2 * self.bit[j]) * 2 * 2**j for j in range(self.bits)]
+        self.partner = self.ctx + 1 - 2 * self.core
+        self.orders = (list(range(self.bits)), list(reversed(range(self.bits))))
+
+    def at(self, free=(), other=None):
+        return tuple(
+            slice(None) if j in free else (1 - self.bit[j] if j == other else self.bit[j])
+            for j in reversed(range(self.bits))
+        )
+
+    def barrier(self, plane=True, line=True, near=False):
+        sem = pltpu.get_barrier_semaphore()
+        count = 0
+        if plane:
+            for p in self.across + [self.partner]:
+                pl.semaphore_signal(sem, inc=1, device_id={"ctx": p}, device_id_type=MESH)
+                count += 1
+        if line:
+            for k in range(1, self.fsdp_count):
+                pl.semaphore_signal(
+                    sem,
+                    inc=1,
+                    device_id={"fsdp": (self.z + k) % self.fsdp_count},
+                    device_id_type=MESH,
+                )
+                count += 1
+        pl.semaphore_wait(sem, count)
+
+
+def remote(src, dst, send, recv, **where):
+    return pltpu.make_async_remote_copy(
+        src, dst, send, recv, device_id=where, device_id_type=MESH
+    )
+
+
+def run_ticks(jobs, spacing=SPACING):
+    depth = max(len(job) for job in jobs)
+    for tick in range(len(jobs) + spacing * (depth - 1)):
+        for j in reversed(range(depth)):
+            t = tick - spacing * j
+            if 0 <= t < len(jobs) and j < len(jobs[t]):
+                jobs[t][j]()
+
+
+def column_half(ref, half):
+    n = ref.shape[-1] // 2
+    return pl.ds(half * n, n)
+
+
+def gather_kernel(nf, nc, count, *refs):
+    shards, small = refs[:count], refs[count]
+    outs, small_out = refs[count + 1 : 2 * count + 1], refs[2 * count + 1]
+    stages = refs[2 * count + 2 : 3 * count + 3]
+    up_s, up_r, down_s, down_r, ps, pr, cs, cr, ss, sr, load_sem, store_sem = refs[3 * count + 3 :]
+    me = Place(nc, nf)
+    z = me.z
+    loads = [
+        pltpu.make_async_copy(src, dst, load_sem.at[i])
+        for i, (src, dst) in enumerate(zip(list(shards) + [small], stages))
+    ]
+    stores = [
+        pltpu.make_async_copy(stages[i], dst.at[z], store_sem.at[i])
+        for i, dst in enumerate(list(outs) + [small_out])
+    ]
+    for load in loads:
+        load.start()
+    me.barrier()
+
+    def source(k):
+        pairs = jnp.minimum(z, nf - 1 - z)
+        near = (k + 1) // 2
+        near_source = z - near if k % 2 == 1 else z + near
+        far = k - pairs
+        far_source = jnp.where(2 * z < nf - 1, z + far, z - far)
+        return jnp.where(k <= 2 * pairs, near_source, far_source)
+
+    sources = [None] + [source(k) for k in range(1, nf)]
+
+    def line_copy(i, src_z, src, up):
+        to = z + 1 if up else z - 1
+        sems = (up_s, up_r) if up else (down_s, down_r)
+        return remote(
+            src,
+            outs[i].at[(src_z, me.core) + me.at()],
+            sems[0].at[i, src_z],
+            sems[1].at[i, src_z],
+            fsdp=to,
+        )
+
+    def line_start(i, src_z, src, up, condition):
+        @pl.when(condition)
+        def _():
+            line_copy(i, src_z, src, up).start()
+
+    def small_copy(k):
+        return remote(small, small_out.at[z], ss.at[k], sr.at[k], fsdp=(z + k) % nf)
+
+    for k in range(1, nf):
+        small_copy(k).start()
+    for i in range(count):
+        mine = shards[i].at[(me.core,) + me.at()]
+        line_start(i, z, mine, True, z + 1 < nf)
+        line_start(i, z, mine, False, z > 0)
+
+    def line_stage(i, k):
+        src_z = sources[k]
+        here = outs[i].at[(src_z, me.core) + me.at()]
+        below = src_z < z
+
+        @pl.when(below)
+        def _():
+            line_copy(i, src_z, here, True).wait_recv()
+
+        @pl.when(jnp.logical_not(below))
+        def _():
+            line_copy(i, src_z, here, False).wait_recv()
+
+        line_start(i, src_z, here, True, jnp.logical_and(below, z + 1 < nf))
+        line_start(i, src_z, here, False, jnp.logical_and(src_z > z, z > 0))
+
+    def plane_copy(i, k, half, j):
+        order = me.orders[half]
+        ref = outs[i].at[
+            (sources[k], me.core) + me.at(order[:j]) + (slice(None), column_half(outs[i], half))
+        ]
+        return remote(
+            ref, ref, ps.at[half, i, k, j], pr.at[half, i, k, j], ctx=me.across[order[j]]
+        )
+
+    def core_copy(i, k):
+        ref = outs[i].at[sources[k], me.core]
+        return remote(ref, ref, cs.at[i, k], cr.at[i, k], ctx=me.partner)
+
+    def plane_stage(i, k, j):
+        if j == 0:
+            line_stage(i, k)
+        else:
+            for half in (0, 1):
+                plane_copy(i, k, half, j - 1).wait_recv()
+        if j < me.bits:
+            for half in (0, 1):
+                plane_copy(i, k, half, j).start()
+        else:
+            core_copy(i, k).start()
+
+    order = [(i, k) for i in range(count) for k in range(1, nf)]
+    jobs = [
+        [functools.partial(plane_stage, i, k, j) for j in range(me.bits + 1)]
+        + [core_copy(i, k).wait_recv]
+        for i, k in order
+    ]
+    for load, store in zip(loads, stores):
+        load.wait()
+        store.start()
+    run_ticks(jobs)
+    for k in range(1, nf):
+        small_copy(k).wait_recv()
+        small_copy(k).wait_send()
+    for i in range(count):
+        @pl.when(z + 1 < nf)
+        def _():
+            line_copy(i, z, shards[i].at[(me.core,) + me.at()], True).wait_send()
+
+        @pl.when(z > 0)
+        def _():
+            line_copy(i, z, shards[i].at[(me.core,) + me.at()], False).wait_send()
+
+    for i, k in order:
+        src_z = sources[k]
+        here = outs[i].at[(src_z, me.core) + me.at()]
+
+        @pl.when(jnp.logical_and(src_z < z, z + 1 < nf))
+        def _():
+            line_copy(i, src_z, here, True).wait_send()
+
+        @pl.when(jnp.logical_and(src_z > z, z > 0))
+        def _():
+            line_copy(i, src_z, here, False).wait_send()
+
+        for half in (0, 1):
+            for j in range(me.bits):
+                plane_copy(i, k, half, j).wait_send()
+        core_copy(i, k).wait_send()
+    for store in stores:
+        store.wait()
+
+
+def gather_weights(nf, nc, shards, small):
+    _, bits = plane_shape(nc)
+    count = len(shards)
+    views = [w.reshape((2,) * (1 + bits) + (w.shape[0] // nc, w.shape[1])) for w in shards]
+    arrays = views + [small]
+    outs = pl.pallas_call(
+        functools.partial(gather_kernel, nf, nc, count),
+        out_shape=[jax.ShapeDtypeStruct((nf,) + v.shape, v.dtype) for v in arrays],
+        in_specs=[HBM_SPEC] * (count + 1),
+        out_specs=[HBM_SPEC] * (count + 1),
+        scratch_shapes=[pltpu.VMEM(v.shape, v.dtype) for v in arrays]
+        + [DMA((count, nf))] * 4
+        + [DMA((2, count, nf, bits))] * 2
+        + [DMA((count, nf))] * 2
+        + [DMA((nf,))] * 2
+        + [DMA((count + 1,))] * 2,
+        compiler_params=pltpu.CompilerParams(collective_id=0, has_side_effects=True),
+        name="gather_weights",
+    )(*arrays)
+    return [o.reshape(nf * w.shape[0], w.shape[1]) for o, w in zip(outs, shards)], outs[count]
+
+
+def gather_pair_kernel(nf, nc, pair, out, stage, ps, pr, cs, cr, load_sem, store_sem):
+    me = Place(nc, nf)
+    load = pltpu.make_async_copy(pair, stage, load_sem)
+    load.start()
+    me.barrier(line=False)
+
+    def plane_copy(half, j):
+        order = me.orders[half]
+        where = (slice(None), column_half(out, half))
+        dst = out.at[me.at(order[:j]) + (me.core,) + where]
+        src = pair.at[where] if j == 0 else dst
+        return remote(src, dst, ps.at[half, j], pr.at[half, j], ctx=me.across[order[j]])
+
+    own_core = remote(pair, out.at[me.at() + (me.core,)], cs.at[0, 0], cr.at[0, 0], ctx=me.partner)
+
+    def core_copy(half, j):
+        order = me.orders[half]
+        ref = out.at[
+            me.at(order[:j], other=order[j]) + (me.core, slice(None), column_half(out, half))
+        ]
+        return remote(ref, ref, cs.at[half, j + 1], cr.at[half, j + 1], ctx=me.partner)
+
+    for half in (0, 1):
+        plane_copy(half, 0).start()
+    own_core.start()
+    load.wait()
+    store = pltpu.make_async_copy(stage, out.at[me.at() + (me.core,)], store_sem)
+    store.start()
+    store.wait()
+    for j in range(me.bits):
+        for half in (0, 1):
+            plane_copy(half, j).wait_recv()
+        if j + 1 < me.bits:
+            for half in (0, 1):
+                plane_copy(half, j + 1).start()
+        for half in (0, 1):
+            core_copy(half, j).start()
+    own_core.wait()
+    for j in range(me.bits):
+        for half in (0, 1):
+            plane_copy(half, j).wait_send()
+            core_copy(half, j).wait()
+
+
+def gather_pair(nf, nc, pair):
+    _, bits = plane_shape(nc)
+    out = pl.pallas_call(
+        functools.partial(gather_pair_kernel, nf, nc),
+        out_shape=jax.ShapeDtypeStruct((2,) * (bits + 1) + pair.shape, pair.dtype),
+        in_specs=[HBM_SPEC],
+        out_specs=HBM_SPEC,
+        scratch_shapes=[pltpu.VMEM(pair.shape, pair.dtype)]
+        + [DMA((2, bits))] * 2
+        + [DMA((2, bits + 1))] * 2
+        + [DMA, DMA],
+        compiler_params=pltpu.CompilerParams(collective_id=1, has_side_effects=True),
+        name="gather_pair",
+    )(pair)
+    return out.reshape(nc * pair.shape[0], pair.shape[1])
+
+
+def scatter_pair_kernel(nf, nc, grads, out, held, core_in, *refs):
+    _, bits = plane_shape(nc)
+    ins = refs[: 2 * bits]
+    cs, cr, ps, pr, load_sem = refs[2 * bits :]
+    me = Place(nc, nf)
+    every = tuple(slice(None) for _ in range(bits))
+    load = pltpu.make_async_copy(grads.at[every + (me.core,)], held, load_sem)
+    load.start()
+    me.barrier(line=False)
+    core_copy = remote(
+        grads.at[every + (1 - me.core,)], core_in, cs, cr, ctx=me.partner
+    )
+    core_copy.start()
+    load.wait()
+    core_copy.wait_recv()
+    rows, width = held.shape[-2:]
+    halves = [pl.ds(0, width // 2), pl.ds(width // 2, width // 2)]
+
+    def add(index, source, source_index, cols):
+        held[index + (slice(None), cols)] = (
+            held[index + (slice(None), cols)].astype(jnp.float32)
+            + source[source_index].astype(jnp.float32)
+        ).astype(held.dtype)
+
+    def every_chip(free):
+        todo = [()]
+        for j in reversed(range(bits)):
+            todo = [t + (v,) for t in todo for v in ((0, 1) if j in free else (me.bit[j],))]
+        return todo
+
+    def plane_copy(half, j):
+        order = me.orders[half]
+        src = held.at[me.at(order[j + 1 :], other=order[j]) + (slice(None), halves[half])]
+        return remote(
+            src, ins[2 * j + half], ps.at[half, j], pr.at[half, j], ctx=me.across[order[j]]
+        )
+
+    for index in every_chip(range(bits)):
+        add(index, core_in, index, pl.ds(0, width))
+    for half in (0, 1):
+        plane_copy(half, 0).start()
+    for j in range(bits):
+        for half in (0, 1):
+            order = me.orders[half]
+            plane_copy(half, j).wait_recv()
+            free = order[j + 1 :]
+            todo = [()]
+            for b in reversed(range(bits)):
+                if b in free:
+                    todo = [t + (v,) for t in todo for v in (0, 1)]
+            for chip, part in zip(every_chip(free), todo):
+                add(chip, ins[2 * j + half], part, halves[half])
+            if j + 1 < bits:
+                plane_copy(half, j + 1).start()
+    out[...] = held[me.at()]
+    core_copy.wait_send()
+    for j in range(bits):
+        for half in (0, 1):
+            plane_copy(half, j).wait_send()
+
+
+def scatter_pair(nf, nc, grads):
+    chips, bits = plane_shape(nc)
+    rows, width = grads.shape[0] // nc, grads.shape[1]
+    view = grads.reshape((2,) * (bits + 1) + (rows, width))
+    return pl.pallas_call(
+        functools.partial(scatter_pair_kernel, nf, nc),
+        out_shape=jax.ShapeDtypeStruct((rows, width), grads.dtype),
+        in_specs=[HBM_SPEC],
+        out_specs=pl.BlockSpec(memory_space=pltpu.VMEM),
+        scratch_shapes=[pltpu.VMEM((2,) * bits + (rows, width), grads.dtype)] * 2
+        + [
+            pltpu.VMEM((2,) * (bits - 1 - j) + (rows, width // 2), grads.dtype)
+            for j in range(bits)
+            for _ in (0, 1)
+        ]
+        + [DMA, DMA]
+        + [DMA((2, bits))] * 2
+        + [DMA],
+        compiler_params=pltpu.CompilerParams(collective_id=2, has_side_effects=True),
+        name="scatter_pair",
+    )(view)
+
+
+def reduce_kernel(nf, nc, count, *refs):
+    _, bits = plane_shape(nc)
+    parts, small = refs[:count], refs[count]
+    outs, small_out = refs[count + 1 : 2 * count + 1], refs[2 * count + 1]
+    rest = list(refs[2 * count + 2 :])
+    held = [rest.pop(0) for _ in range(count)]
+    ins = [[[rest.pop(0) for _ in (0, 1)] for _ in range(bits)] for _ in range(count)]
+    line_in = [rest.pop(0) for _ in range(count)]
+    final = [rest.pop(0) for _ in range(count)]
+    small_sum, small_in, small_line = rest.pop(0), rest.pop(0), rest.pop(0)
+    (load_sem, ps, pr, ls, lr, gs, gr, cs, cr, own_sem, ss, sr, sls, slr) = rest
+    me = Place(nc, nf)
+    z = me.z
+    loads = [pltpu.make_async_copy(parts[i], held[i], load_sem.at[i]) for i in range(count)]
+    for load in loads:
+        load.start()
+    me.barrier()
+
+    def target(k):
+        return (z + k) % nf
+
+    def plane_copy(i, k, half, j):
+        order = me.orders[half]
+        ref = parts[i] if j == 0 else held[i]
+        src = ref.at[
+            (target(k),)
+            + me.at(order[j + 1 :], other=order[j])
+            + (slice(None), column_half(ref, half))
+        ]
+        return remote(
+            src,
+            ins[i][j][half].at[k],
+            ps.at[half, i, k, j],
+            pr.at[half, i, k, j],
+            ctx=me.across[order[j]],
+        )
+
+    def chips_of(free):
+        places, local = [()], [()]
+        for b in reversed(range(bits)):
+            if b in free:
+                places = [t + (v,) for t in places for v in (0, 1)]
+                local = [t + (v,) for t in local for v in (0, 1)]
+            else:
+                places = [t + (me.bit[b],) for t in places]
+        return list(zip(places, local))
+
+    def add(i, k, half, j):
+        free = me.orders[half][j + 1 :]
+        rows, width = held[i].shape[-2], held[i].shape[-1] // 2
+        step = min(rows, 32)
+        cols = pl.ds(half * width, width)
+        for place, local in chips_of(free):
+
+            def body(t, carry, place=place, local=local):
+                at = pl.ds(pl.multiple_of(t * step, step), step)
+                where = (target(k),) + place + (at, cols)
+                total = held[i][where].astype(jnp.float32) + ins[i][j][half][
+                    (k,) + local + (at,)
+                ].astype(jnp.float32)
+                held[i][where] = total.astype(held[i].dtype)
+                return carry
+
+            lax.fori_loop(0, rows // step, body, 0)
+
+    def line_copy(i, k):
+        return remote(
+            held[i].at[(target(k),) + me.at()],
+            line_in[i].at[k],
+            ls.at[i, k],
+            lr.at[i, k],
+            fsdp=target(k),
+        )
+
+    def stage(i, k, j):
+        if j > 0:
+            for half in (0, 1):
+                plane_copy(i, k, half, j - 1).wait_recv()
+                add(i, k, half, j - 1)
+        if j < bits:
+            for half in (0, 1):
+                plane_copy(i, k, half, j).start()
+        elif k != 0:
+            line_copy(i, k).start()
+
+    def own_copy(i):
+        return pltpu.make_async_copy(final[i], outs[i].at[(me.core,) + me.at()], own_sem.at[i])
+
+    def gather_copy(i, half, j):
+        order = me.orders[half]
+        cols = column_half(final[i], half)
+        dst = outs[i].at[(me.core,) + me.at(order[:j]) + (slice(None), cols)]
+        src = final[i].at[:, cols] if j == 0 else dst
+        return remote(
+            src, dst, gs.at[half, i, j], gr.at[half, i, j], ctx=me.across[order[j]]
+        )
+
+    def core_copy(i):
+        ref = outs[i].at[me.core]
+        return remote(ref, ref, cs.at[i], cr.at[i], ctx=me.partner)
+
+    def total(i):
+        for k in range(1, nf):
+            line_copy(i, k).wait_recv()
+        rows = final[i].shape[0]
+        step = min(rows, 32)
+
+        def body(t, carry):
+            at = pl.ds(pl.multiple_of(t * step, step), step)
+            value = held[i][(z,) + me.at() + (at,)].astype(jnp.float32)
+            for k in range(1, nf):
+                value = value + line_in[i][k, at].astype(jnp.float32)
+            final[i][at] = value.astype(final[i].dtype)
+            return carry
+
+        lax.fori_loop(0, rows // step, body, 0)
+        own_copy(i).start()
+
+    def gather_stage(i, j):
+        if j == 0:
+            own_copy(i).wait()
+        else:
+            for half in (0, 1):
+                gather_copy(i, half, j - 1).wait_recv()
+        if j < bits:
+            for half in (0, 1):
+                gather_copy(i, half, j).start()
+        else:
+            core_copy(i).start()
+
+    across = [me.partner] + me.across
+
+    def small_copy(s):
+        return remote(small_sum.at[s], small_in.at[s], ss.at[s], sr.at[s], ctx=across[s])
+
+    def small_line_copy(k):
+        return remote(
+            small_sum.at[bits + 1], small_line.at[z], sls.at[k], slr.at[k], fsdp=target(k)
+        )
+
+    def small_stage(s):
+        if s > 0:
+            small_copy(s - 1).wait_recv()
+            small_sum[s] = small_sum[s - 1] + small_in[s - 1]
+        if s <= bits:
+            small_copy(s).start()
+        else:
+            for k in range(1, nf):
+                small_line_copy(k).start()
+            small_line[z] = small_sum[s]
+
+    small_sum[0] = small[...]
+    jobs = []
+    for i in range(count):
+        for k in list(range(1, nf)) + [0]:
+            job = [functools.partial(stage, i, k, j) for j in range(bits + 1)]
+            if k == 0:
+                job += [functools.partial(total, i)]
+                job += [functools.partial(gather_stage, i, j) for j in range(bits + 1)]
+                job += [core_copy(i).wait_recv]
+            jobs.append(job)
+    small_job = [functools.partial(small_stage, s) for s in range(bits + 2)]
+    for load in loads:
+        load.wait()
+    run_ticks([small_job] + jobs)
+    for k in range(1, nf):
+        small_line_copy(k).wait_recv()
+    value = small_line[0]
+    for k in range(1, nf):
+        value = value + small_line[k]
+    small_out[...] = value
+    for s in range(bits + 1):
+        small_copy(s).wait_send()
+    for k in range(1, nf):
+        small_line_copy(k).wait_send()
+    for i in range(count):
+        for k in range(nf):
+            for half in (0, 1):
+                for j in range(bits):
+                    plane_copy(i, k, half, j).wait_send()
+            if k:
+                line_copy(i, k).wait_send()
+        for half in (0, 1):
+            for j in range(bits):
+                gather_copy(i, half, j).wait_send()
+        core_copy(i).wait_send()
+
+
+def reduce_gradients(nf, nc, parts, small):
+    _, bits = plane_shape(nc)
+    count = len(parts)
+    views = [
+        p.reshape((nf,) + (2,) * bits + (p.shape[0] // (nf * 2**bits), p.shape[1])) for p in parts
+    ]
+    pieces = [v.shape[-2:] for v in views]
+    vmem = pl.BlockSpec(memory_space=pltpu.VMEM)
+    outs = pl.pallas_call(
+        functools.partial(reduce_kernel, nf, nc, count),
+        out_shape=[
+            jax.ShapeDtypeStruct((2,) * (bits + 1) + piece, jnp.bfloat16) for piece in pieces
+        ]
+        + [jax.ShapeDtypeStruct(small.shape, jnp.float32)],
+        in_specs=[HBM_SPEC] * count + [vmem],
+        out_specs=[HBM_SPEC] * count + [vmem],
+        scratch_shapes=[pltpu.VMEM(v.shape, jnp.bfloat16) for v in views]
+        + [
+            pltpu.VMEM((nf,) + (2,) * (bits - 1 - j) + (rows, width // 2), jnp.bfloat16)
+            for rows, width in pieces
+            for j in range(bits)
+            for _ in (0, 1)
+        ]
+        + [pltpu.VMEM((nf,) + piece, jnp.bfloat16) for piece in pieces]
+        + [pltpu.VMEM(piece, jnp.bfloat16) for piece in pieces]
+        + [
+            pltpu.VMEM((bits + 2,) + small.shape, jnp.float32),
+            pltpu.VMEM((bits + 1,) + small.shape, jnp.float32),
+            pltpu.VMEM((nf,) + small.shape, jnp.float32),
+        ]
+        + [DMA((count,))]
+        + [DMA((2, count, nf, bits))] * 2
+        + [DMA((count, nf))] * 2
+        + [DMA((2, count, bits))] * 2
+        + [DMA((count,))] * 2
+        + [DMA((count,))]
+        + [DMA((bits + 1,))] * 2
+        + [DMA((nf,))] * 2,
+        compiler_params=pltpu.CompilerParams(collective_id=3, has_side_effects=True),
+        name="reduce_gradients",
+    )(*views, small)
+    return [
+        o.reshape(p.shape[0] // nf * 2, p.shape[1]) for o, p in zip(outs, parts)
+    ], outs[count]
 
 
 def per_device(
@@ -89,22 +702,18 @@
     ctx_count = lax.axis_size("ctx")
     fsdp_count = lax.axis_size("fsdp")
     ctx_rank = lax.axis_index("ctx")
-    qkv_full, out_full, attn_gathered, qk_gathered = (
-        lax.all_gather(query_key_value_weight, "fsdp", axis=0, tiled=True),
-        lax.all_gather(w_out, "fsdp", axis=0, tiled=True),
-        lax.all_gather(gain_attn, "fsdp", axis=0, tiled=True),
-        lax.all_gather(gain_qk, "fsdp", axis=1, tiled=True),
-    )
-    gate_full, up_full, down_full, ffn_gathered = (
-        lax.all_gather(w_gate, "fsdp", axis=0, tiled=True),
-        lax.all_gather(w_up, "fsdp", axis=0, tiled=True),
-        lax.all_gather(w_down, "fsdp", axis=0, tiled=True),
-        lax.all_gather(gain_ffn, "fsdp", axis=0, tiled=True),
-    )
-    attn_gain = attn_gathered.astype(jnp.float32)
-    ffn_gain = ffn_gathered.astype(jnp.float32)
-    query_gain = qk_gathered[0].astype(jnp.float32)
-    key_gain = qk_gathered[1].astype(jnp.float32)
+    model_shard = gain_attn.shape[0]
+    qk_shard = gain_qk.shape[1]
+    gains = pack_rows([gain_attn, gain_ffn, gain_qk], 8)
+    (qkv_full, out_full, gate_full, up_full, down_full), gains = gather_weights(
+        fsdp_count, ctx_count, [query_key_value_weight, w_out, w_gate, w_up, w_down], gains
+    )
+    gains = gains.reshape(fsdp_count, -1)
+    attn_gain = gains[:, :model_shard].reshape(-1)
+    ffn_gain = gains[:, model_shard : 2 * model_shard].reshape(-1)
+    qk_gain = gains[:, 2 * model_shard : 2 * model_shard + 2 * qk_shard]
+    qk_gain = jnp.swapaxes(qk_gain.reshape(fsdp_count, 2, qk_shard), 0, 1).reshape(2, -1)
+    query_gain, key_gain = qk_gain[0], qk_gain[1]
     pack_in = tokens[0].astype(jnp.float32)
     token_rows = pack_in.shape[0]
     block_len = token_rows // 2
@@ -142,7 +751,7 @@
         [key_local.reshape(token_rows, key_value_width), unprojected_value.astype(jnp.bfloat16)],
         axis=1,
     )
-    every_pair = lax.all_gather(local_pair, "ctx", axis=0, tiled=True)
+    every_pair = gather_pair(fsdp_count, ctx_count, local_pair)
     key_block_index = math.gcd(full_len, 512)
     block_total = full_len // key_block_index
     key_block_list = (
@@ -282,11 +891,8 @@
         key_block_list,
     )
     grad_query_rot = query_running.reshape(token_rows, QUERY_HEADS, HEAD_SIZE) * inv_root
-    local_gradients = lax.psum_scatter(
-        pair_grads.reshape(full_len, 2 * key_value_width).astype(jnp.bfloat16),
-        "ctx",
-        scatter_dimension=0,
-        tiled=True,
+    local_gradients = scatter_pair(
+        fsdp_count, ctx_count, pair_grads.reshape(full_len, 2 * key_value_width).astype(jnp.bfloat16)
     ).astype(jnp.float32)
     rotated_key_gradient = local_gradients[:, :key_value_width].reshape(
         token_rows, KEY_VALUE_HEADS, HEAD_SIZE
@@ -310,75 +916,73 @@
     grad_input_part, attn_gain_part = norm_backward(pack_in, attn_inverse, attn_gain, grad_normed)
     tokens_grad = grad_resid + grad_input_part
 
-    def arrange(values):
-        leading = values.shape[:-1]
-        last_len = values.shape[-1]
-        split_view = values.reshape(
-            leading + (fsdp_count, ctx_count, last_len // (fsdp_count * ctx_count))
-        )
-        return jnp.swapaxes(split_view, -3, -2).reshape(leading + (last_len,))
-
-    qk_sum = jnp.stack([jnp.sum(query_gain_part, axis=(0, 1)), jnp.sum(key_gain_part, axis=(0, 1))])
-    qk_major = jnp.transpose(
-        qk_sum.reshape(2, fsdp_count, HEAD_SIZE // fsdp_count), (1, 0, 2)
-    ).reshape(2 * HEAD_SIZE)
-    grad_qkv = transposed_times(arrange(normed_low), grad_projected)
-    grad_out = transposed_times(arrange(attended), grad_branch)
-    grad_wgate = transposed_times(arrange(normed_ffn_low), grad_gate)
-    grad_wup = transposed_times(arrange(normed_ffn_low), grad_up)
-    grad_wdown = transposed_times(arrange(hidden), grad_mixed)
-    grad_attn_gain = arrange(jnp.sum(attn_gain_part, axis=0))
-    grad_ffn_gain = arrange(jnp.sum(ffn_gain_part, axis=0))
-    grad_qk_gain = arrange(qk_major)
-    pieces = (
-        lax.psum_scatter(grad_qkv, ("ctx", "fsdp"), scatter_dimension=0, tiled=True),
-        lax.psum_scatter(grad_out, ("ctx", "fsdp"), scatter_dimension=0, tiled=True),
-        lax.psum_scatter(grad_wgate, ("ctx", "fsdp"), scatter_dimension=0, tiled=True),
-        lax.psum_scatter(grad_wup, ("ctx", "fsdp"), scatter_dimension=0, tiled=True),
-        lax.psum_scatter(grad_wdown, ("ctx", "fsdp"), scatter_dimension=0, tiled=True),
-        lax.psum_scatter(grad_attn_gain, ("ctx", "fsdp"), scatter_dimension=0, tiled=True),
-        lax.psum_scatter(grad_ffn_gain, ("ctx", "fsdp"), scatter_dimension=0, tiled=True),
-        lax.psum_scatter(grad_qk_gain, ("ctx", "fsdp"), scatter_dimension=0, tiled=True),
-    )
-    totals = (
-        lax.all_gather(pieces[0].astype(jnp.bfloat16), "ctx", axis=0, tiled=True).astype(
-            jnp.float32
-        ),
-        lax.all_gather(pieces[1].astype(jnp.bfloat16), "ctx", axis=0, tiled=True).astype(
-            jnp.float32
-        ),
-        lax.all_gather(pieces[2].astype(jnp.bfloat16), "ctx", axis=0, tiled=True).astype(
-            jnp.float32
-        ),
-        lax.all_gather(pieces[3].astype(jnp.bfloat16), "ctx", axis=0, tiled=True).astype(
-            jnp.float32
-        ),
-        lax.all_gather(pieces[4].astype(jnp.bfloat16), "ctx", axis=0, tiled=True).astype(
-            jnp.float32
-        ),
-        lax.all_gather(pieces[5].astype(jnp.bfloat16), "ctx", axis=0, tiled=True).astype(
-            jnp.float32
-        ),
-        lax.all_gather(pieces[6].astype(jnp.bfloat16), "ctx", axis=0, tiled=True).astype(
-            jnp.float32
-        ),
-        lax.all_gather(pieces[7].astype(jnp.bfloat16), "ctx", axis=0, tiled=True).astype(
-            jnp.float32
-        ),
-    )
-    qk_shard = totals[7].reshape(2, HEAD_SIZE // fsdp_count)
+    core = ctx_rank % 2
+    swap = [(i, i + 1 - 2 * (i % 2)) for i in range(ctx_count)]
+
+    def both(values):
+        return jnp.concatenate([values, lax.ppermute(values, "ctx", swap)], axis=0)
+
+    def core_part(values, which):
+        view = values.reshape(token_rows, fsdp_count, 2, -1)
+        return lax.dynamic_index_in_dim(view, which, 2, keepdims=False).reshape(token_rows, -1)
+
+    def both_part(values):
+        mine = core_part(values, core)
+        other = lax.ppermute(core_part(values, 1 - core), "ctx", swap)
+        return jnp.concatenate([mine, other], axis=0)
+
+    ffn_rows = both_part(normed_ffn_low)
+    parts = [
+        transposed_times(left, right).astype(jnp.bfloat16)
+        for left, right in (
+            (both_part(hidden), both(grad_mixed)),
+            (ffn_rows, both(grad_gate)),
+            (ffn_rows, both(grad_up)),
+            (both_part(attended), both(grad_branch)),
+            (both_part(normed_low), both(grad_projected)),
+        )
+    ]
+    gain_sums = pack_rows(
+        [
+            jnp.sum(attn_gain_part, axis=0),
+            jnp.sum(ffn_gain_part, axis=0),
+            jnp.sum(query_gain_part, axis=(0, 1)),
+            jnp.sum(key_gain_part, axis=(0, 1)),
+        ],
+        8,
+    )
+    (down_grad, gate_grad, up_grad, out_grad, qkv_grad), gain_sums = reduce_gradients(
+        fsdp_count, ctx_count, parts, gain_sums
+    )
+    gain_sums = gain_sums.reshape(-1)
+    model = model_shard * fsdp_count
+    rank = lax.axis_index("fsdp")
+    attn_gain_grad = lax.dynamic_slice_in_dim(gain_sums, rank * model_shard, model_shard)
+    ffn_gain_grad = lax.dynamic_slice_in_dim(gain_sums, model + rank * model_shard, model_shard)
+    qk_gain_grad = lax.dynamic_slice_in_dim(
+        gain_sums[2 * model : 2 * model + 2 * HEAD_SIZE].reshape(2, HEAD_SIZE),
+        rank * qk_shard,
+        qk_shard,
+        axis=1,
+    )
     return (
         mixed_out[None],
         tokens_grad[None],
-        totals[0],
-        totals[1],
-        totals[2],
-        totals[3],
-        totals[4],
-        totals[5],
-        totals[6],
-        qk_shard,
-    )
+        qkv_grad.astype(jnp.float32),
+        out_grad.astype(jnp.float32),
+        gate_grad.astype(jnp.float32),
+        up_grad.astype(jnp.float32),
+        down_grad.astype(jnp.float32),
+        attn_gain_grad,
+        ffn_gain_grad,
+        qk_gain_grad,
+    )
+
+
+def pack_rows(arrays, multiple):
+    flat = jnp.concatenate([a.astype(jnp.float32).reshape(-1) for a in arrays])
+    size = multiple * 128
+    return jnp.pad(flat, (0, -flat.shape[0] % size)).reshape(-1, 128)
 
 
 def solution(mesh):

time: 1680 us -> 590 us (0.35)
  waiting for transfers between devices: 1250 us -> 0.02 us
  Pallas kernels: 0 us -> 268 us
  blocking collectives: 82.3 us -> 0 us
    reduce_scatter x6 -> x0, waiting for transfers between devices: 873 us -> none  [the longest x1 184 us: per_device(): lax.psum_scatter(grad_wdown, ('ctx', 'fsdp'), scatter_dimension=0, tiled=...]
    all_gather x11 -> x0, waiting for transfers between devices: 375 us -> none  [the longest x1 85.3 us: per_device(): lax.all_gather(query_key_value_weight, 'fsdp', axis=0, tiled=True)]
    pallas_call x0 -> x4, Pallas kernels: none -> 268 us  [the longest x1 133 us: reduce_gradients(): pl.pallas_call(functools.partial(reduce_kernel, nf, nc, count), out_shape...]
    unnamed x2 -> x0, blocking collectives: 53.9 us -> none
    all_gather x3 -> x0, blocking collectives: 28.4 us -> none  [the longest x1 10.4 us: per_device(): lax.all_gather(gain_attn, 'fsdp', axis=0, tiled=True)]
  transfers between devices with their start and end apart: 17 -> 9, of which waited for: 13 -> 0; matrix products, arithmetic and copies ran while one was open for 12% -> 49% of each run, Pallas kernels for 0% -> 23%
where the time goes in v1:
time: 590 us; the launch traced here: 584 us
  Pallas kernels  268 us (45%)
  matrix products  178 us (30%)
  local copies, waits for them, and re-layouts  66.5 us (11%)
  other arithmetic  65.4 us (11%)
    pallas_call x1, Pallas kernels, reduce_gradients(): pl.pallas_call(functools.partial(reduce_kernel, nf, nc, count), out_shape...  133 us
    pallas_call x1, Pallas kernels, gather_weights(): pl.pallas_call(functools.partial(gather_kernel, nf, nc, count), out_shape...  102 us
    dot_general x12, matrix products, block_scores(): jnp.einsum('qkgd,tkd->kgqt', grouped_heads, key_tile, preferred_element_t...  40.4 us
    unnamed x150, local copies, waits for them, and re-layouts  21.9 us
    dot_general x5, matrix products, times_transposed(): lax.dot_general(left, right, (((1,), (1,)), ((), ())), preferred_element_...  21.1 us
    reduce_sum x4, other arithmetic, stats_step(): jnp.sum(jnp.exp(scores - new_max[..., None]), axis=-1)  20.3 us
    dot_general x4, matrix products, gradient_update(): jnp.einsum('kgqt,qkgd->tkd', soft_probs.astype(jnp.bfloat16), grouped_gra...  19.7 us
    dot_general x4, matrix products, output_update(): jnp.einsum('kgqt,tkd->qkgd', soft_probs, tiles[3], preferred_element_type...  19.4 us
  transfers between devices with their start and end apart: 9, of which 0 were waited for; matrix products, arithmetic and copies ran while one was open for 49% of the time, Pallas kernels for 23%

profile of v1, /device:TPU:1, one launch (start us, length us, event | category | flops | bytes accessed | tf_op | source)
XLA Modules:
  0.0 583.9 jit_solution(5103322062735655954)
XLA Ops:
  2.8 102.2 %gather_weights.1 = (bf16[4,2,2,2,64,1536]{5,4,3,2,1,0:T(8,128)(2,1)}, bf16[4,2,2,2,32,2048]{5,4,3,2,1,0:T(8,128)(2,1)}, bf16[4,2,2,2,64,1024]{5,4,3,2,1,0:T(8,1...) custom-call(bf16[2,2,2,64,1536]{4,3,2,1,0:T(8,128)(2,1)} %bitcast.42, ...), custom_call_target="tpu_custom_call" | custom-call | tf_op jit(solution)/shard_map/gather_weights/pallas_call | solution.py:292
  106.6 4.6 fusion.92
  114.6 4.4 compare_select_fusion.1
  119.2 5.6 fusion.115
  126.3 15.6 %gather_pair.1 = bf16[2,2,2,256,512]{4,3,2,1,0:T(8,128)(2,1)} custom-call(bf16[256,512]{1,0:T(8,128)(2,1)} %pad_maximum_fusion.6.pair), custom_call_target="tpu_custom_call" | custom-call | tf_op jit(solution)/shard_map/gather_pair/pallas_call | solution.py:355
  141.9 2.6 fusion.138
  146.8 4.4 reshape.855
  151.2 2.9 copy.84
  156.9 40.2 %while.49 = (s32[]{:T(128)}, f32[4,4,256]{2,1,0:T(4,128)S(1)}, f32[4,4,256]{2,1,0:T(4,128)S(1)}, s32[256]{0:T(256)S(1)}, s32[4,512]{1,0:T(4,128)S(1)}, /*index=5...) while((s32[]{:T(128)}, f32[4,4,256]{2,1,0:T(4,128)S(1)}, ...), condition=%wide.region_7.8_spmd.clone, body=%wide.region_4.7_spmd.clone.sunk | while | flops 283529216 | bytes 18184328 | solution.py:792
  157.2 4.7 fusion.203
  161.9 5.1 exponential_reduce_fusion.2
  167.2 4.7 fusion.203
  171.9 5.1 exponential_reduce_fusion.2
  177.3 4.7 fusion.203
  182.0 5.1 exponential_reduce_fusion.2
  187.3 4.7 fusion.203
  192.0 5.1 exponential_reduce_fusion.2
  197.1 20.5 %while.50 = (s32[]{:T(128)}, f32[256,4,4,64]{0,3,2,1:T(8,128)}, bf16[4,512,4,64]{1,3,2,0:T(8,128)(2,1)S(1)}, s32[256]{0:T(256)S(1)}, s32[4,512]{1,0:T(4,128)S(1)...) while((s32[]{:T(128)}, f32[256,4,4,64]{0,3,2,1:T(8,128)}, ...), condition=%wide.region_9.10_spmd.clone, body=%wide.region_8.9_spmd.clone.sunk | while | flops 548274176 | bytes 3456658 | solution.py:810
  197.4 3.9 fusion.209
  201.5 5.2 fusion.209
  206.9 5.2 fusion.209
  212.3 5.2 fusion.209
  220.0 3.7 multiply_reduce_fusion.2
  229.6 3.0 multiply_convert_fusion.2
  232.7 2.6 reshape.738
  235.3 5.1 constant_dynamic-slice_fusion.14
  240.4 3.7 copy.130
  244.7 5.0 fusion.144
  249.6 5.4 multiply_reduce_fusion
  259.9 22.5 %while.51 = (s32[]{:T(128)}, f32[4,4,256]{2,1,0:T(4,128)S(1)}, s32[256]{0:T(256)S(1)}, s32[4,512]{1,0:T(4,128)S(1)}, s32[4,512]{1,0:T(4,128)S(1)}, /*index=5*/s3...) while((s32[]{:T(128)}, f32[4,4,256]{2,1,0:T(4,128)S(1)}, ...), condition=%wide.region_14.15_spmd.clone, body=%wide.region_12.14_spmd.clone.sunk | while | flops 549851136 | bytes 18725024 | solution.py:850
  262.5 3.1 fusion.215
  268.1 3.1 fusion.215
  273.7 3.1 fusion.215
  279.3 3.1 fusion.215
  282.5 69.8 %while.52 = (s32[]{:T(128)}, f32[256,4,4,64]{0,3,2,1:T(8,128)S(1)}, bf16[4,512,512]{1,2,0:T(8,128)(2,1)}, bf16[4,512,4,64]{1,3,2,0:T(8,128)(2,1)S(1)}, s32[256]{...) while((s32[]{:T(128)}, f32[256,4,4,64]{0,3,2,1:T(8,128)S(1)}, ...), condition=%wide.region_16.17_spmd.clone, body=%wide.region_15.16_spmd.clone.sunk | while | flops 1361182720 | bytes 94959864 | solution.py:888
  283.2 2.3 fusion.226
  285.5 4.5 fusion.227
  290.1 3.1 fusion.228
  293.2 4.9 fusion.229
  300.5 2.3 fusion.226
  302.9 4.5 fusion.227
  307.4 3.1 fusion.228
  310.5 4.9 fusion.229
  317.9 2.3 fusion.226
  320.2 4.5 fusion.227
  324.8 3.1 fusion.228
  327.9 4.9 fusion.229
  337.6 4.5 fusion.227
  342.1 3.1 fusion.228
  345.2 4.9 fusion.229
  352.3 4.3 copy.95
  356.7 16.8 %scatter_pair.1 = bf16[256,512]{1,0:T(8,128)(2,1)} custom-call(bf16[2,2,2,256,512]{4,3,2,1,0:T(8,128)(2,1)} %bitcast.408), custom_call_target="tpu_custom_call" | custom-call | tf_op jit(solution)/shard_map/scatter_pair/pallas_call | solution.py:435
  381.9 2.5 multiply_reduce_fusion.3
  386.4 6.5 %fusion.79 = (f32[2048]{0:T(1024)S(1)}, f32[256]{0:T(256)S(1)}, f32[256,2048]{1,0:T(8,128)}) fusion(bf16[1,256,2048]{2,1,0:T(8,128)(2,1)S(1)} %copy-done.8, f32[256]{0:T(256)S(1)} %copy-done.59, f32[2048]{0:T(1024)S(1)} %bitcast.460, bf16[2048,1536]{1,0:T(8,128)(2,1)} %bitcast.470, bf16[256,256]{1,0:T(8,128)(2,1)S(1)} %copy-done.41, ...), kind=kOutput, calls=%fused_computation.106 | convolution fusion | flops 1616639744 | bytes 10242048 | tf_op jit(solution)/shard_map/dot_general | solution.py:21
  397.4 3.1 reshape.757
  400.5 4.1 copy.106
  404.6 5.2 fusion.76
  417.8 4.0 convolution_convert_fusion.4
  421.8 4.0 convolution_convert_fusion.3
  426.3 4.7 convolution_convert_fusion
  431.0 3.8 convolution_convert_fusion.2
  434.8 2.6 convolution_convert_fusion.1
  437.4 133.3 %reduce_gradients.1 = (bf16[2,2,2,32,2048]{4,3,2,1,0:T(8,128)(2,1)}, bf16[2,2,2,64,1024]{4,3,2,1,0:T(8,128)(2,1)}, bf16[2,2,2,64,1024]{4,3,2,1,0:T(8,128)(2,1)},...) custom-call(bf16[4,2,2,32,2048]{4,3,2,1,0:T(8,128)(2,1)} %bitcast.422, ...), custom_call_target="tpu_custom_call" | custom-call | tf_op jit(solution)/shard_map/reduce_gradients/pallas_call | solution.py:650
  570.8 3.6 bitcast_convert_fusion
  (343 shorter events, 83.4 us)
Async XLA Ops:
  0.6 430.3 %collective-permute-start.1 = (bf16[256,2048]{1,0:T(8,128)(2,1)}, bf16[256,2048]{1,0:T(8,128)(2,1)}, u32[]{:S(2)}, u32[]{:S(2)}) collective-permute-start(bf16[256,2048]{1,0:T(8,128)(2,1)} %bitcast.413), channel_id=1, source_target_pairs={{0,4},{4,0},{8,12},{12,8},{16,20},{20,16},{24,28},{28,24},{1,5},{5... | collective-permute-start | bytes 3145736 | tf_op jit(solution)/shard_map/ppermute | solution.py:923
  2.8 103.5 %copy-start.6 = (bf16[1,256,2048]{2,1,0:T(8,128)(2,1)S(1)}, bf16[1,256,2048]{2,1,0:T(8,128)(2,1)}, u32[]{:S(2)}) copy-start(bf16[1,256,2048]{2,1,0:T(8,128)(2,1)} %param.22) | copy-start | bytes 3145732
  106.3 4.9 copy-start.54
  106.6 4.6 copy-start.58
  111.3 2.6 copy-start.49
  111.3 13.6 %copy-start.68 = (s32[1,8]{1,0:T(1,128)S(1)}, s32[1,8]{1,0:T(1,128)}, u32[]{:S(2)}) copy-start(s32[1,8]{1,0:T(1,128)} %param.24) | copy-start | bytes 100
  113.7 11.5 %copy-start.62 = (f32[64]{0:T(128)}, f32[64]{0:T(128)S(1)}, u32[]{:S(2)}) copy-start(f32[64]{0:T(128)S(1)} %mul.548) | copy-start | bytes 772
  113.8 28.1 %copy-start.27 = (f32[256,256]{0,1:T(8,128)}, f32[256,256]{0,1:T(8,128)S(1)}, u32[]{:S(2)}) copy-start(f32[256,256]{0,1:T(8,128)S(1)} %copy.77) | copy-start | bytes 786436
  113.9 11.3 %copy-start.50 = (f32[256,4]{0,1:T(4,128)}, f32[256,4]{0,1:T(4,128)S(1)}, u32[]{:S(2)}) copy-start(f32[256,4]{0,1:T(4,128)S(1)} %add_rsqrt_fusion.1) | copy-start | bytes 12292
  125.4 30.8 %copy-start.37 = (f32[256,32]{0,1:T(8,128)}, f32[256,32]{0,1:T(8,128)S(1)}, u32[]{:S(2)}) copy-start(f32[256,32]{0,1:T(8,128)S(1)} %get-tuple-element.731) | copy-start | bytes 98308
  125.4 30.8 %copy-start.39 = (f32[256,32]{0,1:T(8,128)}, f32[256,32]{0,1:T(8,128)S(1)}, u32[]{:S(2)}) copy-start(f32[256,32]{0,1:T(8,128)S(1)} %get-tuple-element.732) | copy-start | bytes 98308
  217.7 2.3 copy-start.7
  219.8 3.9 copy-start.16
  219.8 35.3 %copy-start.45 = (f32[1,4,4,128]{3,1,2,0:T(4,128)}, f32[1,4,4,128]{3,1,2,0:T(4,128)S(1)}, u32[]{:S(2)}) copy-start(f32[1,4,4,128]{3,1,2,0:T(4,128)S(1)} %copy.139) | copy-start | bytes 24580
  220.0 4.0 copy-start.71
  223.7 31.4 %copy-start.2 = (f32[256,2048]{1,0:T(8,128)}, f32[256,2048]{1,0:T(8,128)S(1)}, u32[]{:S(2)}) copy-start(f32[256,2048]{1,0:T(8,128)S(1)} %get-tuple-element.750) | copy-start | bytes 6291460
  223.7 31.3 %copy-start.56 = (f32[256]{0:T(256)}, f32[256]{0:T(256)S(1)}, u32[]{:S(2)}) copy-start(f32[256]{0:T(256)S(1)} %add_rsqrt_fusion.2) | copy-start | bytes 3076
  224.0 3.0 copy-start.22
  227.0 2.5 copy-start.69
  232.5 183.2 %collective-permute-start.3 = (bf16[256,1024]{1,0:T(8,128)(2,1)}, bf16[256,1024]{1,0:T(8,128)(2,1)}, u32[]{:S(2)}, u32[]{:S(2)}) collective-permute-start(bf16[256,1024]{1,0:T(8,128)(2,1)} %get-tuple-element.700), channel_id=1, source_target_pairs={{0,4},{4,0},{8,12},{12,8},{16,20},{20,16},{24,28},{28,24},{1,5},{5... | collective-permute-start | bytes 1572872 | tf_op jit(solution)/shard_map/ppermute | solution.py:923
  244.1 172.5 %collective-permute-start.2 = (bf16[256,1024]{0,1:T(8,128)(2,1)}, bf16[256,1024]{0,1:T(8,128)(2,1)}, u32[]{:S(2)}, u32[]{:S(2)}) collective-permute-start(bf16[256,1024]{0,1:T(8,128)(2,1)} %bitcast.61), channel_id=1, source_target_pairs={{0,4},{4,0},{8,12},{12,8},{16,20},{20,16},{24,28},{28,24},{1,5},{5... | collective-permute-start | bytes 1572872 | tf_op jit(solution)/shard_map/ppermute | solution.py:931
  244.5 177.2 %collective-permute-start.4 = (bf16[256,1024]{1,0:T(8,128)(2,1)}, bf16[256,1024]{1,0:T(8,128)(2,1)}, u32[]{:S(2)}, u32[]{:S(2)}) collective-permute-start(bf16[256,1024]{1,0:T(8,128)(2,1)} %get-tuple-element.699), channel_id=1, source_target_pairs={{0,4},{4,0},{8,12},{12,8},{16,20},{20,16},{24,28},{28,24},{1,5},{5... | collective-permute-start | bytes 1572872 | tf_op jit(solution)/shard_map/ppermute | solution.py:923
  249.6 5.5 copy-start.24
  255.1 3.3 copy-start.13
  259.9 22.6 %copy-start.4 = (f32[256,4,4,64]{0,3,2,1:T(8,128)S(1)}, f32[256,4,4,64]{0,3,2,1:T(8,128)}, u32[]{:S(2)}) copy-start(f32[256,4,4,64]{0,3,2,1:T(8,128)} %custom-call.4) | copy-start | bytes 3145732
  285.5 4.5 copy-start.1
  293.2 4.9 copy-start
  302.9 4.5 copy-start.1
  310.5 4.9 copy-start
  320.2 4.5 copy-start.1
  327.8 4.9 copy-start
  337.6 4.5 copy-start.1
  345.2 4.9 copy-start
  356.6 18.5 %copy-start.51 = (f32[256,4]{0,1:T(4,128)S(1)}, f32[256,4]{0,1:T(4,128)}, u32[]{:S(2)}) copy-start(f32[256,4]{0,1:T(4,128)} %copy-done.50) | copy-start | bytes 12292
  356.6 18.8 %copy-start.38 = (f32[256,32]{0,1:T(8,128)S(1)}, f32[256,32]{0,1:T(8,128)}, u32[]{:S(2)}) copy-start(f32[256,32]{0,1:T(8,128)} %copy-done.37) | copy-start | bytes 98308
  356.6 18.8 %copy-start.40 = (f32[256,32]{0,1:T(8,128)S(1)}, f32[256,32]{0,1:T(8,128)}, u32[]{:S(2)}) copy-start(f32[256,32]{0,1:T(8,128)} %copy-done.39) | copy-start | bytes 98308
  356.6 18.8 %copy-start.28 = (f32[256,256]{0,1:T(8,128)S(1)}, f32[256,256]{0,1:T(8,128)}, u32[]{:S(2)}) copy-start(f32[256,256]{0,1:T(8,128)} %copy-done.27) | copy-start | bytes 786436
  356.7 18.8 %copy-start.63 = (f32[64]{0:T(128)S(1)}, f32[64]{0:T(128)}, u32[]{:S(2)}) copy-start(f32[64]{0:T(128)} %copy-done.62) | copy-start | bytes 772
  381.8 2.5 copy-start.41
  381.8 4.5 copy-start.8
  381.8 4.5 copy-start.55
  381.8 4.5 copy-start.59
  384.3 8.6 %copy-start.29 = (bf16[256,1024]{1,0:T(8,128)(2,1)}, bf16[256,1024]{1,0:T(8,128)(2,1)S(1)}, u32[]{:S(2)}) copy-start(bf16[256,1024]{1,0:T(8,128)(2,1)S(1)} %get-tuple-element.696) | copy-start | bytes 1572868
  385.3 7.5 %copy-start.3 = (f32[256,2048]{1,0:T(8,128)S(1)}, f32[256,2048]{1,0:T(8,128)}, u32[]{:S(2)}) copy-start(f32[256,2048]{1,0:T(8,128)} %copy-done.2) | copy-start | bytes 6291460
  385.3 7.5 %copy-start.42 = (bf16[256,1024]{1,0:T(8,128)(2,1)S(1)}, bf16[256,1024]{1,0:T(8,128)(2,1)}, u32[]{:S(2)}) copy-start(bf16[256,1024]{1,0:T(8,128)(2,1)} %get-tuple-element.701) | copy-start | bytes 1572868
  385.3 7.5 %copy-start.70 = (bf16[4,2,2,2,32,2048]{5,4,3,2,1,0:T(8,128)(2,1)S(1)}, bf16[4,2,2,2,32,2048]{5,4,3,2,1,0:T(8,128)(2,1)}, u32[]{:S(2)}) copy-start(bf16[4,2,2,2,32,2048]{5,4,3,2,1,0:T(8,128)(2,1)} %get-tuple-element.282) | copy-start | bytes 12582916
  385.3 40.9 %collective-permute-start.8 = (bf16[256,1536]{1,0:T(8,128)(2,1)}, bf16[256,1536]{1,0:T(8,128)(2,1)}, u32[]{:S(2)}, u32[]{:S(2)}) collective-permute-start(bf16[256,1536]{1,0:T(8,128)(2,1)} %pad_maximum_fusion.2), channel_id=1, source_target_pairs={{0,4},{4,0},{8,12},{12,8},{16,20},{20,16},{24,28},{28,24},{1,5},{5... | collective-permute-start | bytes 2359304 | tf_op jit(solution)/shard_map/ppermute | solution.py:923
  400.5 4.2 copy-start.46
  400.5 4.2 copy-start.57
  400.5 4.2 copy-start.61
  404.6 5.3 copy-start.15
  404.6 5.2 copy-start.52
  410.9 3.3 copy-start.21
  412.0 3.6 copy-start.53
  414.2 3.5 copy-start.17
  416.6 18.2 %collective-permute-start.6 = (bf16[256,2048]{1,0:T(8,128)(2,1)S(1)}, bf16[256,2048]{1,0:T(8,128)(2,1)S(1)}, u32[]{:S(2)}, u32[]{:S(2)}) collective-permute-start(bf16[256,2048]{1,0:T(8,128)(2,1)S(1)} %copy-done.36), channel_id=1, source_target_pairs={{0,4},{4,0},{8,12},{12,8},{16,20},{20,16},{24,28},{28,24},{1,5},{5... | collective-permute-start | bytes 3145736 | tf_op jit(solution)/shard_map/ppermute | solution.py:923
  416.6 9.2 %collective-permute-start.7 = (bf16[256,1024]{0,1:T(8,128)(2,1)S(1)}, bf16[256,1024]{0,1:T(8,128)(2,1)S(1)}, u32[]{:S(2)}, u32[]{:S(2)}) collective-permute-start(bf16[256,1024]{0,1:T(8,128)(2,1)S(1)} %bitcast.439), channel_id=1, source_target_pairs={{0,4},{4,0},{8,12},{12,8},{16,20},{20,16},{24,28},{28,24},{1,5},{5... | collective-permute-start | bytes 1572872 | tf_op jit(solution)/shard_map/ppermute | solution.py:931
  417.8 4.0 copy-start.44
  421.8 4.5 copy-start.30
  421.8 9.2 %collective-permute-start = (bf16[256,512]{0,1:T(8,128)(2,1)S(1)}, bf16[256,512]{0,1:T(8,128)(2,1)S(1)}, u32[]{:S(2)}, u32[]{:S(2)}) collective-permute-start(bf16[256,512]{0,1:T(8,128)(2,1)S(1)} %bitcast.441), channel_id=1, source_target_pairs={{0,4},{4,0},{8,12},{12,8},{16,20},{20,16},{24,28},{28,24},{1,5},{5... | collective-permute-start | bytes 786440 | tf_op jit(solution)/shard_map/ppermute | solution.py:931
  425.8 9.0 %collective-permute-start.5 = (bf16[256,512]{0,1:T(8,128)(2,1)S(1)}, bf16[256,512]{0,1:T(8,128)(2,1)S(1)}, u32[]{:S(2)}, u32[]{:S(2)}) collective-permute-start(bf16[256,512]{0,1:T(8,128)(2,1)S(1)} %bitcast.443), channel_id=1, source_target_pairs={{0,4},{4,0},{8,12},{12,8},{16,20},{20,16},{24,28},{28,24},{1,5},{5... | collective-permute-start | bytes 786440 | tf_op jit(solution)/shard_map/ppermute | solution.py:931
  426.3 4.7 copy-start.25
  426.3 4.7 copy-start.43
  570.8 3.6 copy-start.34
  (23 other events, 30.8 us)

commit v2 on v1

--- a/solution.py
+++ b/solution.py
@@ -1,5 +1,4 @@
 import functools
-import math
 
 import jax
 import jax.numpy as jnp
@@ -15,65 +14,6 @@
 
 EPSILON = 1e-06
 THETA = 10000.0
-
-
-def times_transposed(left, right):
-    return lax.dot_general(
-        left, right, (((1,), (1,)), ((), ())), preferred_element_type=jnp.float32
-    )
-
-
-def transposed_times(left, right):
-    return lax.dot_general(
-        left, right, (((0,), (0,)), ((), ())), preferred_element_type=jnp.float32
-    )
-
-
-def norm_forward(values, gain_vec):
-    inverse = lax.rsqrt(jnp.mean(values * values, axis=-1, keepdims=True) + EPSILON)
-    return (values * inverse * gain_vec, inverse)
-
-
-def norm_backward(values, inverse, gain_vec, grad_out):
-    scaled = grad_out * gain_vec
-    grad_in = inverse * (
-        scaled - values * inverse * inverse * jnp.mean(scaled * values, axis=-1, keepdims=True)
-    )
-    return (grad_in, grad_out * values * inverse)
-
-
-def rotate(values, cosines, sine_vals):
-    half_dim = values.shape[-1] // 2
-    first_half = values[..., :half_dim]
-    second_half = values[..., half_dim:]
-    return jnp.concatenate(
-        [
-            first_half * cosines - second_half * sine_vals,
-            second_half * cosines + first_half * sine_vals,
-        ],
-        axis=-1,
-    )
-
-
-def rotate_back(grad_out, cosines, sine_vals):
-    half_dim = grad_out.shape[-1] // 2
-    first_half = grad_out[..., :half_dim]
-    second_half = grad_out[..., half_dim:]
-    return jnp.concatenate(
-        [
-            first_half * cosines + second_half * sine_vals,
-            second_half * cosines - first_half * sine_vals,
-        ],
-        axis=-1,
-    )
-
-
-def rotary_tables(position, doc_begin):
-    offsets = (position - doc_begin).astype(jnp.float32)
-    frequency = THETA ** (-jnp.arange(0, HEAD_SIZE // 2, dtype=jnp.float32) * 2.0 / HEAD_SIZE)
-    angles = offsets[:, None] * frequency[None, :]
-    return (jnp.cos(angles)[:, None, :], jnp.sin(angles)[:, None, :])
-
 
 MESH = pl.DeviceIdType.MESH
 DMA = pltpu.SemaphoreType.DMA
@@ -685,6 +625,496 @@
     ], outs[count]
 
 
+LANES = 128
+GROUP = QUERY_HEADS // KEY_VALUE_HEADS
+SMEM_SPEC = pl.BlockSpec(memory_space=pltpu.SMEM)
+VMEM_SPEC = pl.BlockSpec(memory_space=pltpu.VMEM)
+
+
+def low_lanes(shape):
+    return lax.broadcasted_iota(jnp.int32, shape, len(shape) - 1) % LANES < HEAD_SIZE
+
+
+def stack_heads(ref, row, group, length, high):
+    tiles = []
+    for pair in range(GROUP // 2):
+        cols = pl.ds((group * GROUP // 2 + pair) * LANES, LANES)
+        tile = ref[pl.ds(row, length), cols].astype(jnp.float32)
+        turned = pltpu.roll(tile, HEAD_SIZE, 1)
+        low = low_lanes(tile.shape)
+        if high:
+            tiles += [jnp.where(low, 0.0, turned), jnp.where(low, 0.0, tile)]
+        else:
+            tiles += [jnp.where(low, tile, 0.0), jnp.where(low, turned, 0.0)]
+    return jnp.concatenate(tiles, axis=0)
+
+
+def unstack_heads(ref, row, group, length, value, high):
+    for pair in range(GROUP // 2):
+        cols = pl.ds((group * GROUP // 2 + pair) * LANES, LANES)
+        first = value[2 * pair * length : (2 * pair + 1) * length]
+        second = value[(2 * pair + 1) * length : (2 * pair + 2) * length]
+        low = low_lanes(first.shape)
+        if high:
+            tile = jnp.where(low, pltpu.roll(first, HEAD_SIZE, 1), second)
+        else:
+            tile = jnp.where(low, first, pltpu.roll(second, HEAD_SIZE, 1))
+        ref[pl.ds(row, length), cols] = tile.astype(ref.dtype)
+
+
+def query_span(rank, order, starts, stored_of, which, length):
+    block = order[2 * rank + which]
+    first = jnp.int32(0)
+    place = block * length + lax.broadcasted_iota(jnp.int32, (1, length), 1)
+    begin = jnp.zeros((1, length), jnp.int32)
+    for d in range(starts.shape[1]):
+        first = jnp.where(starts[0, d] <= block * length, starts[0, d], first)
+        begin = jnp.where(starts[0, d] <= place, starts[0, d], begin)
+    place = jnp.concatenate([place] * GROUP, axis=1)
+    begin = jnp.concatenate([begin] * GROUP, axis=1)
+    return block, first // length, place, begin
+
+
+def invert_order(order, stored_of):
+    for s in range(order.shape[0]):
+        stored_of[order[s]] = s
+
+
+def key_rows(stored_of, block, length, blocks):
+    second = stored_of[jnp.minimum(block + 1, blocks - 1)]
+    return [
+        pl.ds(pl.multiple_of(s * length, length), length) for s in (stored_of[block], second)
+    ]
+
+
+def allowed_keys(block, place, begin, length):
+    key = block * length + lax.broadcasted_iota(jnp.int32, (2 * length, place.shape[1]), 0)
+    return (key >= begin) & (key <= place)
+
+
+def dot_last(left, right):
+    return lax.dot_general(
+        left, right, (((1,), (1,)), ((), ())), preferred_element_type=jnp.float32
+    )
+
+
+def dot_plain(left, right):
+    return lax.dot_general(
+        left, right, (((1,), (0,)), ((), ())), preferred_element_type=jnp.float32
+    )
+
+
+def attend_kernel(rank, order, starts, query, pair, attended, exact, log_sum, stored_of, acc, queries):
+    length = query.shape[0] // 2
+    blocks = order.shape[0]
+    invert_order(order, stored_of)
+
+    def one_block(which, carry):
+        row = pl.multiple_of(which * length, length)
+        block, first, place, begin = query_span(rank[0], order, starts, stored_of, which, length)
+        for g in range(KEY_VALUE_HEADS):
+            queries[g] = stack_heads(query, row, g, length, False).astype(jnp.bfloat16)
+        acc[...] = jnp.zeros_like(acc)
+
+        def step(t, carry):
+            key_block = first + 2 * t
+            rows = key_rows(stored_of, key_block, length, blocks)
+            allowed = allowed_keys(key_block, place, begin, length)
+            for g in range(KEY_VALUE_HEADS):
+                cols = pl.ds(g * LANES, LANES)
+                keys = jnp.concatenate([pair[r, cols] for r in rows], axis=0)
+                scores = dot_last(keys, queries[g])
+                weights = jnp.where(allowed, jnp.exp(scores), 0.0).astype(jnp.bfloat16)
+                ones = jnp.where(low_lanes(keys.shape), 1.0, keys.astype(jnp.float32))
+                acc[g] += dot_plain(ones.T.astype(jnp.bfloat16), weights)
+            return carry
+
+        lax.fori_loop(0, (block - first + 2) // 2, step, 0)
+        for g in range(KEY_VALUE_HEADS):
+            total = acc[g]
+            sums = total[0:1]
+            log_sum[which, g] = jnp.broadcast_to(jnp.log(sums), log_sum.shape[2:])
+            value = (total / sums).T
+            unstack_heads(attended, row, g, length, value, True)
+            unstack_heads(exact, row, g, length, value, True)
+        return carry
+
+    lax.fori_loop(0, 2, one_block, 0)
+
+
+def attend(rank, order, starts, query, pair):
+    rows = query.shape[0]
+    wide = GROUP * (rows // 2)
+    return pl.pallas_call(
+        attend_kernel,
+        out_shape=[
+            jax.ShapeDtypeStruct(query.shape, jnp.bfloat16),
+            jax.ShapeDtypeStruct(query.shape, jnp.float32),
+            jax.ShapeDtypeStruct((2, KEY_VALUE_HEADS, 8, wide), jnp.float32),
+        ],
+        in_specs=[SMEM_SPEC] * 3 + [VMEM_SPEC] * 2,
+        out_specs=[VMEM_SPEC] * 3,
+        scratch_shapes=[
+            pltpu.SMEM((order.shape[0],), jnp.int32),
+            pltpu.VMEM((KEY_VALUE_HEADS, LANES, wide), jnp.float32),
+            pltpu.VMEM((KEY_VALUE_HEADS, wide, LANES), jnp.bfloat16),
+        ],
+        name="attend",
+    )(rank, order, starts, query, pair)
+
+
+def attend_back_kernel(
+    rank, order, starts, query, pair, grad, exact, log_sum, grad_query, grad_pair,
+    stored_of, total, acc, queries, grads, delta,
+):
+    length = query.shape[0] // 2
+    blocks = order.shape[0]
+    invert_order(order, stored_of)
+    total[...] = jnp.zeros_like(total)
+
+    def one_block(which, carry):
+        row = pl.multiple_of(which * length, length)
+        block, first, place, begin = query_span(rank[0], order, starts, stored_of, which, length)
+        for g in range(KEY_VALUE_HEADS):
+            queries[g] = stack_heads(query, row, g, length, False).astype(jnp.bfloat16)
+            upper = stack_heads(grad, row, g, length, True)
+            grads[g] = upper.astype(jnp.bfloat16)
+            product = upper * stack_heads(exact, row, g, length, True)
+            delta[g] = jnp.broadcast_to(
+                jnp.sum(product.T, axis=0, keepdims=True), delta.shape[1:]
+            )
+        acc[...] = jnp.zeros_like(acc)
+
+        def step(t, carry):
+            key_block = first + 2 * t
+            rows = key_rows(stored_of, key_block, length, blocks)
+            allowed = allowed_keys(key_block, place, begin, length)
+            for g in range(KEY_VALUE_HEADS):
+                cols = pl.ds(g * LANES, LANES)
+                keys = jnp.concatenate([pair[r, cols] for r in rows], axis=0)
+                scores = dot_last(keys, queries[g])
+                probs = jnp.where(allowed, jnp.exp(scores - log_sum[which, g, 0:1]), 0.0)
+                grad_probs = dot_last(keys, grads[g])
+                grad_scores = (probs * (grad_probs - delta[g, 0:1])).astype(jnp.bfloat16)
+                turned = keys.astype(jnp.float32).T.astype(jnp.bfloat16)
+                acc[g] += dot_plain(turned, grad_scores)
+                both = dot_plain(grad_scores, queries[g]) + dot_plain(
+                    probs.astype(jnp.bfloat16), grads[g]
+                )
+                total[rows[0], cols] += both[:length]
+                total[rows[1], cols] += both[length:]
+            return carry
+
+        lax.fori_loop(0, (block - first + 2) // 2, step, 0)
+        for g in range(KEY_VALUE_HEADS):
+            unstack_heads(grad_query, row, g, length, acc[g].T, False)
+        return carry
+
+    lax.fori_loop(0, 2, one_block, 0)
+
+    def finish(t, carry):
+        at = pl.ds(pl.multiple_of(t * length, length), length)
+        grad_pair[at, :] = total[at, :].astype(grad_pair.dtype)
+        return carry
+
+    lax.fori_loop(0, blocks, finish, 0)
+
+
+def attend_back(rank, order, starts, query, pair, grad, exact, log_sum):
+    rows = query.shape[0]
+    wide = GROUP * (rows // 2)
+    return pl.pallas_call(
+        attend_back_kernel,
+        out_shape=[
+            jax.ShapeDtypeStruct(query.shape, jnp.float32),
+            jax.ShapeDtypeStruct(pair.shape, jnp.bfloat16),
+        ],
+        in_specs=[SMEM_SPEC] * 3 + [VMEM_SPEC] * 5,
+        out_specs=[VMEM_SPEC] * 2,
+        scratch_shapes=[
+            pltpu.SMEM((order.shape[0],), jnp.int32),
+            pltpu.VMEM(pair.shape, jnp.float32),
+            pltpu.VMEM((KEY_VALUE_HEADS, LANES, wide), jnp.float32),
+            pltpu.VMEM((KEY_VALUE_HEADS, wide, LANES), jnp.bfloat16),
+            pltpu.VMEM((KEY_VALUE_HEADS, wide, LANES), jnp.bfloat16),
+            pltpu.VMEM((KEY_VALUE_HEADS, 8, wide), jnp.float32),
+        ],
+        name="attend_back",
+    )(rank, order, starts, query, pair, grad, exact, log_sum)
+
+
+CHUNK = 256
+
+
+def head_means(values):
+    shape = (LANES, LANES)
+    same = (
+        lax.broadcasted_iota(jnp.int32, shape, 0) // HEAD_SIZE
+        == lax.broadcasted_iota(jnp.int32, shape, 1) // HEAD_SIZE
+    )
+    ones = jnp.where(same, 1.0, 0.0).astype(jnp.bfloat16)
+    high = values.astype(jnp.bfloat16)
+    low = (values - high.astype(jnp.float32)).astype(jnp.bfloat16)
+    return (dot_plain(high, ones) + dot_plain(low, ones)) * (1.0 / HEAD_SIZE)
+
+
+def first_quarter(shape):
+    return lax.broadcasted_iota(jnp.int32, shape, len(shape) - 1) % HEAD_SIZE < HEAD_SIZE // 2
+
+
+def turn(values, cosines, sines, sign):
+    half = HEAD_SIZE // 2
+    ahead = pltpu.roll(values, LANES - half, 1)
+    behind = pltpu.roll(values, half, 1)
+    other = jnp.where(first_quarter(values.shape), -ahead, behind)
+    return values * cosines + sign * other * sines
+
+
+def row_inverse(ref, rows):
+    total = jnp.zeros((rows, 1), jnp.float32)
+    width = ref.shape[1]
+    for j in range(0, width, CHUNK):
+        value = ref[:, j : j + CHUNK].astype(jnp.float32)
+        total = total + jnp.sum(value * value, axis=1, keepdims=True)
+    return lax.rsqrt(total * (1.0 / width) + EPSILON)
+
+
+def project_kernel(
+    rank, order, starts, tokens, weight, gain, qk_gain, frequency,
+    normed, raw, query, pair, cosines, sines,
+):
+    rows = tokens.shape[0]
+    length = rows // 2
+    for which in (0, 1):
+        block = order[2 * rank[0] + which]
+        place = block * length + lax.broadcasted_iota(jnp.int32, (length, LANES), 0)
+        begin = jnp.zeros((length, LANES), jnp.int32)
+        for d in range(starts.shape[1]):
+            begin = jnp.where(starts[0, d] <= place, starts[0, d], begin)
+        angle = (place - begin).astype(jnp.float32) * frequency[...]
+        at = pl.ds(which * length, length)
+        cosines[at, :] = jnp.cos(angle)
+        sines[at, :] = jnp.sin(angle)
+    inverse = row_inverse(tokens, rows)
+    for j in range(0, tokens.shape[1], CHUNK):
+        cols = pl.ds(j, CHUNK)
+        value = tokens[:, cols].astype(jnp.float32) * inverse * gain[:, cols]
+        normed[:, cols] = value.astype(jnp.bfloat16)
+    query_width = QUERY_HEADS * HEAD_SIZE
+    key_width = KEY_VALUE_HEADS * HEAD_SIZE
+
+    def head_turn(cols, which):
+        value = raw[:, cols]
+        scale = lax.rsqrt(head_means(value * value) + EPSILON)
+        return turn(value * scale * qk_gain[which : which + 1, :], cosines[...], sines[...], 1.0)
+
+    for j in range(0, weight.shape[1], CHUNK):
+        raw[:, j : j + CHUNK] = dot_plain(normed[...], weight[:, j : j + CHUNK])
+    for j in range(0, query_width, LANES):
+        cols = pl.ds(j, LANES)
+        query[:, cols] = (head_turn(cols, 0) * HEAD_SIZE**-0.5).astype(jnp.bfloat16)
+    for j in range(0, key_width, LANES):
+        key = head_turn(pl.ds(query_width + j, LANES), 1)
+        value = raw[:, query_width + key_width + j : query_width + key_width + j + LANES]
+        low = low_lanes(key.shape)
+        first = jnp.where(low, key, pltpu.roll(value, HEAD_SIZE, 1))
+        second = jnp.where(low, pltpu.roll(key, HEAD_SIZE, 1), value)
+        pair[:, 2 * j : 2 * j + LANES] = first.astype(jnp.bfloat16)
+        pair[:, 2 * j + LANES : 2 * j + 2 * LANES] = second.astype(jnp.bfloat16)
+
+
+def project(rank, order, starts, tokens, weight, gain, qk_gain, frequency):
+    rows, width = tokens.shape
+    shape = jax.ShapeDtypeStruct
+    return pl.pallas_call(
+        project_kernel,
+        out_shape=[
+            shape((rows, width), jnp.bfloat16),
+            shape((rows, weight.shape[1]), jnp.float32),
+            shape((rows, QUERY_HEADS * HEAD_SIZE), jnp.bfloat16),
+            shape((rows, 2 * KEY_VALUE_HEADS * HEAD_SIZE), jnp.bfloat16),
+            shape((rows, LANES), jnp.float32),
+            shape((rows, LANES), jnp.float32),
+        ],
+        in_specs=[SMEM_SPEC] * 3 + [VMEM_SPEC] * 5,
+        out_specs=[VMEM_SPEC] * 6,
+        name="project",
+    )(rank, order, starts, tokens, weight, gain, qk_gain, frequency)
+
+
+def feed_kernel(
+    tokens, cotangent, attended, gain, w_out, w_gate, w_up, w_down,
+    mixed, normed, hidden, grad_gate, grad_up, grad_resid, grad_branch, grad_attended, gain_grad,
+    out_v, gate_v, up_v, down_v, resid, sems,
+):
+    rows, width = tokens.shape
+    loads = [
+        pltpu.make_async_copy(src, dst, sems.at[i])
+        for i, (src, dst) in enumerate(
+            ((w_out, out_v), (w_gate, gate_v), (w_up, up_v), (w_down, down_v))
+        )
+    ]
+    for load in loads:
+        load.start()
+    loads[0].wait()
+    for j in range(0, width, CHUNK):
+        cols = pl.ds(j, CHUNK)
+        resid[:, cols] = tokens[:, cols].astype(jnp.float32) + dot_plain(
+            attended[...], out_v[:, cols]
+        )
+    inverse = row_inverse(resid, rows)
+    for j in range(0, width, CHUNK):
+        cols = pl.ds(j, CHUNK)
+        normed[:, cols] = (resid[:, cols] * inverse * gain[:, cols]).astype(jnp.bfloat16)
+    for load in loads[1:]:
+        load.wait()
+    for j in range(0, gate_v.shape[1], CHUNK):
+        cols = pl.ds(j, CHUNK)
+        gate = dot_plain(normed[...], gate_v[:, cols])
+        up = dot_plain(normed[...], up_v[:, cols])
+        sigmoid = 1.0 / (1.0 + jnp.exp(-gate))
+        hidden[:, cols] = (gate * sigmoid * up).astype(jnp.bfloat16)
+        grad_hidden = dot_last(cotangent[...], down_v[cols, :])
+        grad_gate[:, cols] = (
+            grad_hidden * up * sigmoid * (1.0 + gate * (1.0 - sigmoid))
+        ).astype(jnp.bfloat16)
+        grad_up[:, cols] = (grad_hidden * gate * sigmoid).astype(jnp.bfloat16)
+    mean = jnp.zeros((rows, 1), jnp.float32)
+    for j in range(0, width, CHUNK):
+        cols = pl.ds(j, CHUNK)
+        mixed[:, cols] = (resid[:, cols] + dot_plain(hidden[...], down_v[:, cols])).astype(
+            jnp.bfloat16
+        )
+        grad = dot_last(grad_gate[...], gate_v[cols, :]) + dot_last(grad_up[...], up_v[cols, :])
+        grad_resid[:, cols] = grad
+        mean = mean + jnp.sum(grad * gain[:, cols] * resid[:, cols], axis=1, keepdims=True)
+    mean = mean * (1.0 / width) * inverse * inverse
+    for j in range(0, width, CHUNK):
+        cols = pl.ds(j, CHUNK)
+        grad = grad_resid[:, cols]
+        value = resid[:, cols]
+        gain_grad[:, cols] = jnp.sum(grad * value * inverse, axis=0, keepdims=True)
+        total = cotangent[:, cols].astype(jnp.float32) + inverse * (
+            grad * gain[:, cols] - value * mean
+        )
+        grad_resid[:, cols] = total
+        grad_branch[:, cols] = total.astype(jnp.bfloat16)
+    for j in range(0, attended.shape[1], CHUNK):
+        cols = pl.ds(j, CHUNK)
+        grad_attended[:, cols] = dot_last(grad_branch[...], out_v[cols, :]).astype(jnp.bfloat16)
+
+
+def feed(tokens, cotangent, attended, gain, w_out, w_gate, w_up, w_down):
+    rows, width = tokens.shape
+    inner = w_gate.shape[1]
+    shape = jax.ShapeDtypeStruct
+    low, full = jnp.bfloat16, jnp.float32
+    return pl.pallas_call(
+        feed_kernel,
+        out_shape=[
+            shape((rows, width), low),
+            shape((rows, width), low),
+            shape((rows, inner), low),
+            shape((rows, inner), low),
+            shape((rows, inner), low),
+            shape((rows, width), full),
+            shape((rows, width), low),
+            shape(attended.shape, low),
+            shape((1, width), full),
+        ],
+        in_specs=[VMEM_SPEC] * 4 + [HBM_SPEC] * 4,
+        out_specs=[VMEM_SPEC] * 9,
+        scratch_shapes=[pltpu.VMEM(w.shape, low) for w in (w_out, w_gate, w_up, w_down)]
+        + [pltpu.VMEM((rows, width), full), DMA((4,))],
+        name="feed",
+    )(tokens, cotangent, attended, gain, w_out, w_gate, w_up, w_down)
+
+
+def project_back_kernel(
+    tokens, weight, gain, qk_gain, raw, cosines, sines, grad_query, grad_pair, grad_resid,
+    grad_projected, tokens_grad, gain_grad, qk_grad,
+    grads,
+):
+    rows, width = tokens.shape
+    query_width = QUERY_HEADS * HEAD_SIZE
+    key_width = KEY_VALUE_HEADS * HEAD_SIZE
+
+    def head_back(cols, which, grad):
+        grad = turn(grad, cosines[...], sines[...], -1.0)
+        value = raw[:, cols]
+        scale = lax.rsqrt(head_means(value * value) + EPSILON)
+        scaled = grad * qk_gain[which : which + 1, :]
+        mean = head_means(scaled * value)
+        result = scale * (scaled - value * scale * scale * mean)
+        grad_projected[:, cols] = result.astype(jnp.bfloat16)
+        return jnp.sum(grad * value * scale, axis=0, keepdims=True)
+
+    sums = [jnp.zeros((1, LANES), jnp.float32)] * 2
+    for j in range(0, query_width, LANES):
+        cols = pl.ds(j, LANES)
+        sums[0] = sums[0] + head_back(cols, 0, grad_query[:, cols] * HEAD_SIZE**-0.5)
+    for j in range(0, key_width, LANES):
+        first = grad_pair[:, 2 * j : 2 * j + LANES].astype(jnp.float32)
+        second = grad_pair[:, 2 * j + LANES : 2 * j + 2 * LANES].astype(jnp.float32)
+        low = low_lanes(first.shape)
+        key = jnp.where(low, first, pltpu.roll(second, HEAD_SIZE, 1))
+        value = jnp.where(low, pltpu.roll(first, HEAD_SIZE, 1), second)
+        sums[1] = sums[1] + head_back(pl.ds(query_width + j, LANES), 1, key)
+        at = query_width + key_width + j
+        grad_projected[:, at : at + LANES] = value.astype(jnp.bfloat16)
+    for which in (0, 1):
+        qk_grad[which : which + 1, :] = sums[which] + pltpu.roll(sums[which], HEAD_SIZE, 1)
+    inverse = row_inverse(tokens, rows)
+    mean = jnp.zeros((rows, 1), jnp.float32)
+    for j in range(0, width, CHUNK):
+        cols = pl.ds(j, CHUNK)
+        grad = dot_last(grad_projected[...], weight[cols, :])
+        grads[:, cols] = grad
+        value = tokens[:, cols].astype(jnp.float32)
+        mean = mean + jnp.sum(grad * gain[:, cols] * value, axis=1, keepdims=True)
+    mean = mean * (1.0 / width) * inverse * inverse
+    for j in range(0, width, CHUNK):
+        cols = pl.ds(j, CHUNK)
+        grad = grads[:, cols]
+        value = tokens[:, cols].astype(jnp.float32)
+        gain_grad[:, cols] = jnp.sum(grad * value * inverse, axis=0, keepdims=True)
+        tokens_grad[:, cols] = grad_resid[:, cols] + inverse * (
+            grad * gain[:, cols] - value * mean
+        )
+
+
+def project_back(
+    tokens, weight, gain, qk_gain, raw, cosines, sines, grad_query, grad_pair, grad_resid
+):
+    rows, width = tokens.shape
+    shape = jax.ShapeDtypeStruct
+    return pl.pallas_call(
+        project_back_kernel,
+        out_shape=[
+            shape((rows, weight.shape[1]), jnp.bfloat16),
+            shape((rows, width), jnp.float32),
+            shape((1, width), jnp.float32),
+            shape((2, LANES), jnp.float32),
+        ],
+        in_specs=[VMEM_SPEC] * 10,
+        out_specs=[VMEM_SPEC] * 4,
+        scratch_shapes=[pltpu.VMEM((rows, width), jnp.float32)],
+        name="project_back",
+    )(tokens, weight, gain, qk_gain, raw, cosines, sines, grad_query, grad_pair, grad_resid)
+
+
+def transposed_times(left, right):
+    return lax.dot_general(
+        left, right, (((0,), (0,)), ((), ())), preferred_element_type=jnp.float32
+    )
+
+
+def pack_rows(arrays, multiple):
+    flat = jnp.concatenate([a.astype(jnp.float32).reshape(-1) for a in arrays])
+    size = multiple * 128
+    return jnp.pad(flat, (0, -flat.shape[0] % size)).reshape(-1, 128)
+
+
 def per_device(
     tokens,
     cotangent,
@@ -702,220 +1132,59 @@
     ctx_count = lax.axis_size("ctx")
     fsdp_count = lax.axis_size("fsdp")
     ctx_rank = lax.axis_index("ctx")
+    fsdp_rank = lax.axis_index("fsdp")
     model_shard = gain_attn.shape[0]
     qk_shard = gain_qk.shape[1]
+    model = model_shard * fsdp_count
     gains = pack_rows([gain_attn, gain_ffn, gain_qk], 8)
     (qkv_full, out_full, gate_full, up_full, down_full), gains = gather_weights(
         fsdp_count, ctx_count, [query_key_value_weight, w_out, w_gate, w_up, w_down], gains
     )
     gains = gains.reshape(fsdp_count, -1)
-    attn_gain = gains[:, :model_shard].reshape(-1)
-    ffn_gain = gains[:, model_shard : 2 * model_shard].reshape(-1)
+    attn_gain = gains[:, :model_shard].reshape(1, model)
+    ffn_gain = gains[:, model_shard : 2 * model_shard].reshape(1, model)
     qk_gain = gains[:, 2 * model_shard : 2 * model_shard + 2 * qk_shard]
-    qk_gain = jnp.swapaxes(qk_gain.reshape(fsdp_count, 2, qk_shard), 0, 1).reshape(2, -1)
-    query_gain, key_gain = qk_gain[0], qk_gain[1]
-    pack_in = tokens[0].astype(jnp.float32)
+    qk_gain = jnp.swapaxes(qk_gain.reshape(fsdp_count, 2, qk_shard), 0, 1).reshape(2, HEAD_SIZE)
+    qk_gain = jnp.concatenate([qk_gain, qk_gain], axis=1)
+    pack_in = tokens[0]
+    grad_mixed = cotangent[0]
     token_rows = pack_in.shape[0]
-    block_len = token_rows // 2
-    full_len = token_rows * ctx_count
-    key_value_width = KEY_VALUE_HEADS * HEAD_SIZE
-    group_width = QUERY_HEADS // KEY_VALUE_HEADS
-    inv_root = HEAD_SIZE ** (-0.5)
-    start_row = doc_starts[0]
-    stored = jnp.arange(full_len, dtype=jnp.int32)
-    key_place = (
-        jnp.repeat(deal_order, block_len, total_repeat_length=full_len) * block_len
-        + stored % block_len
-    )
-    key_begin = jnp.max(
-        jnp.where(start_row[None, :] <= key_place[:, None], start_row[None, :], 0), axis=1
-    )
-    query_place = lax.dynamic_slice_in_dim(key_place, ctx_rank * token_rows, token_rows)
-    query_begin = lax.dynamic_slice_in_dim(key_begin, ctx_rank * token_rows, token_rows)
-    cosines, sine_vals = rotary_tables(query_place, query_begin)
-    normed, attn_inverse = norm_forward(pack_in, attn_gain)
-    normed_low = normed.astype(jnp.bfloat16)
-    projected_rows = jnp.dot(normed_low, qkv_full, preferred_element_type=jnp.float32)
-    query_raw = projected_rows[:, : QUERY_HEADS * HEAD_SIZE].reshape(
-        token_rows, QUERY_HEADS, HEAD_SIZE
-    )
-    unrotated_key = projected_rows[
-        :, QUERY_HEADS * HEAD_SIZE : (QUERY_HEADS + KEY_VALUE_HEADS) * HEAD_SIZE
-    ].reshape(token_rows, KEY_VALUE_HEADS, HEAD_SIZE)
-    unprojected_value = projected_rows[:, (QUERY_HEADS + KEY_VALUE_HEADS) * HEAD_SIZE :]
-    query_normed, query_inverse = norm_forward(query_raw, query_gain)
-    key_normed, key_inverse = norm_forward(unrotated_key, key_gain)
-    query_heads_rows = rotate(query_normed, cosines, sine_vals).astype(jnp.bfloat16)
-    key_local = rotate(key_normed, cosines, sine_vals).astype(jnp.bfloat16)
-    local_pair = jnp.concatenate(
-        [key_local.reshape(token_rows, key_value_width), unprojected_value.astype(jnp.bfloat16)],
-        axis=1,
-    )
-    every_pair = gather_pair(fsdp_count, ctx_count, local_pair)
-    key_block_index = math.gcd(full_len, 512)
-    block_total = full_len // key_block_index
-    key_block_list = (
-        every_pair[:, :key_value_width].reshape(
-            block_total, key_block_index, KEY_VALUE_HEADS, HEAD_SIZE
-        ),
-        key_place.reshape(block_total, key_block_index),
-        key_begin.reshape(block_total, key_block_index),
-        every_pair[:, key_value_width:].reshape(
-            block_total, key_block_index, KEY_VALUE_HEADS, HEAD_SIZE
-        ),
-    )
-    grouped_heads = query_heads_rows.reshape(token_rows, KEY_VALUE_HEADS, group_width, HEAD_SIZE)
-
-    def block_scores(key_tile, place_tile, begin_tile):
-        raw_scores = (
-            jnp.einsum(
-                "qkgd,tkd->kgqt", grouped_heads, key_tile, preferred_element_type=jnp.float32
-            )
-            * inv_root
-        )
-        allowed = (query_begin[:, None] == begin_tile[None, :]) & (
-            place_tile[None, :] <= query_place[:, None]
-        )
-        return jnp.where(allowed[None, None], raw_scores, -1e30)
-
-    def stats_step(carry, tiles):
-        row_max, row_sum = carry
-        scores = block_scores(tiles[0], tiles[1], tiles[2])
-        new_max = jnp.maximum(row_max, jnp.max(scores, axis=-1))
-        row_sum = row_sum * jnp.exp(row_max - new_max) + jnp.sum(
-            jnp.exp(scores - new_max[..., None]), axis=-1
-        )
-        return ((new_max, row_sum), None)
-
-    initial_maximum = jnp.full((KEY_VALUE_HEADS, group_width, token_rows), -1e30, jnp.float32)
-    initial_sum = jnp.zeros((KEY_VALUE_HEADS, group_width, token_rows), jnp.float32)
-    (row_max, row_sum), unused = lax.scan(
-        stats_step, (initial_maximum, initial_sum), key_block_list
-    )
-
-    def block_probs(tiles):
-        scores = block_scores(tiles[0], tiles[1], tiles[2])
-        return jnp.exp(scores - row_max[..., None]) / row_sum[..., None]
-
-    def output_update(running, tiles):
-        soft_probs = block_probs(tiles).astype(jnp.bfloat16)
-        return (
-            running
-            + jnp.einsum(
-                "kgqt,tkd->qkgd", soft_probs, tiles[3], preferred_element_type=jnp.float32
-            ),
-            None,
-        )
-
-    attended_sum, unused = lax.scan(
-        output_update,
-        jnp.zeros((token_rows, KEY_VALUE_HEADS, group_width, HEAD_SIZE), jnp.float32),
-        key_block_list,
-    )
-    attended = attended_sum.reshape(token_rows, QUERY_HEADS * HEAD_SIZE).astype(jnp.bfloat16)
-    hidden_in = pack_in + jnp.dot(attended, out_full, preferred_element_type=jnp.float32)
-    normed_ffn, ffn_inverse = norm_forward(hidden_in, ffn_gain)
-    normed_ffn_low = normed_ffn.astype(jnp.bfloat16)
-    gate_act = jnp.dot(normed_ffn_low, gate_full, preferred_element_type=jnp.float32)
-    upward = jnp.dot(normed_ffn_low, up_full, preferred_element_type=jnp.float32)
-    sigmoid_gate = jax.nn.sigmoid(gate_act)
-    hidden = (gate_act * sigmoid_gate * upward).astype(jnp.bfloat16)
-    mixed_out = (hidden_in + jnp.dot(hidden, down_full, preferred_element_type=jnp.float32)).astype(
-        jnp.bfloat16
-    )
-    grad_mixed = cotangent[0]
-    grad_hidden = times_transposed(grad_mixed, down_full)
-    grad_gate = (
-        grad_hidden * upward * sigmoid_gate * (1.0 + gate_act * (1.0 - sigmoid_gate))
-    ).astype(jnp.bfloat16)
-    grad_up = (grad_hidden * gate_act * sigmoid_gate).astype(jnp.bfloat16)
-    grad_normed_ffn = times_transposed(grad_gate, gate_full) + times_transposed(grad_up, up_full)
-    grad_resid_part, ffn_gain_part = norm_backward(
-        hidden_in, ffn_inverse, ffn_gain, grad_normed_ffn
-    )
-    grad_resid = grad_mixed.astype(jnp.float32) + grad_resid_part
-    grad_branch = grad_resid.astype(jnp.bfloat16)
-    attended_gradient = times_transposed(grad_branch, out_full).astype(jnp.bfloat16)
-    grouped_gradient = attended_gradient.reshape(
-        token_rows, KEY_VALUE_HEADS, group_width, HEAD_SIZE
-    )
-
-    def delta_update(running, tiles):
-        soft_probs = block_probs(tiles)
-        grad_probs = jnp.einsum(
-            "qkgd,tkd->kgqt", grouped_gradient, tiles[3], preferred_element_type=jnp.float32
-        )
-        return (running + jnp.sum(soft_probs * grad_probs, axis=-1), None)
-
-    row_delta, unused = lax.scan(
-        delta_update,
-        jnp.zeros((KEY_VALUE_HEADS, group_width, token_rows), jnp.float32),
-        key_block_list,
-    )
-
-    def gradient_update(running, tiles):
-        soft_probs = block_probs(tiles)
-        grad_probs = jnp.einsum(
-            "qkgd,tkd->kgqt", grouped_gradient, tiles[3], preferred_element_type=jnp.float32
-        )
-        grad_scores = (soft_probs * (grad_probs - row_delta[..., None])).astype(jnp.bfloat16)
-        running = running + jnp.einsum(
-            "kgqt,tkd->qkgd", grad_scores, tiles[0], preferred_element_type=jnp.float32
-        )
-        grad_keys = (
-            jnp.einsum(
-                "kgqt,qkgd->tkd", grad_scores, grouped_heads, preferred_element_type=jnp.float32
-            )
-            * inv_root
-        )
-        grad_values = jnp.einsum(
-            "kgqt,qkgd->tkd",
-            soft_probs.astype(jnp.bfloat16),
-            grouped_gradient,
-            preferred_element_type=jnp.float32,
-        )
-        return (
-            running,
-            jnp.concatenate(
-                [
-                    grad_keys.reshape(key_block_index, key_value_width),
-                    grad_values.reshape(key_block_index, key_value_width),
-                ],
-                axis=1,
-            ),
-        )
-
-    query_running, pair_grads = lax.scan(
-        gradient_update,
-        jnp.zeros((token_rows, KEY_VALUE_HEADS, group_width, HEAD_SIZE), jnp.float32),
-        key_block_list,
-    )
-    grad_query_rot = query_running.reshape(token_rows, QUERY_HEADS, HEAD_SIZE) * inv_root
-    local_gradients = scatter_pair(
-        fsdp_count, ctx_count, pair_grads.reshape(full_len, 2 * key_value_width).astype(jnp.bfloat16)
-    ).astype(jnp.float32)
-    rotated_key_gradient = local_gradients[:, :key_value_width].reshape(
-        token_rows, KEY_VALUE_HEADS, HEAD_SIZE
-    )
-    grad_value = local_gradients[:, key_value_width:]
-    grad_query, query_gain_part = norm_backward(
-        query_raw, query_inverse, query_gain, rotate_back(grad_query_rot, cosines, sine_vals)
-    )
-    grad_key, key_gain_part = norm_backward(
-        unrotated_key, key_inverse, key_gain, rotate_back(rotated_key_gradient, cosines, sine_vals)
-    )
-    grad_projected = jnp.concatenate(
-        [
-            grad_query.reshape(token_rows, QUERY_HEADS * HEAD_SIZE),
-            grad_key.reshape(token_rows, key_value_width),
-            grad_value,
-        ],
-        axis=1,
-    ).astype(jnp.bfloat16)
-    grad_normed = times_transposed(grad_projected, qkv_full)
-    grad_input_part, attn_gain_part = norm_backward(pack_in, attn_inverse, attn_gain, grad_normed)
-    tokens_grad = grad_resid + grad_input_part
-
+    rank = ctx_rank.reshape(1).astype(jnp.int32)
+    frequency = THETA ** (-jnp.arange(0, HEAD_SIZE // 2, dtype=jnp.float32) * 2.0 / HEAD_SIZE)
+    frequency = jnp.concatenate([frequency] * (2 * LANES // HEAD_SIZE)).reshape(1, LANES)
+
+    normed, raw, query, local_pair, cosines, sines = project(
+        rank, deal_order, doc_starts, pack_in, qkv_full, attn_gain, qk_gain, frequency
+    )
+    pair = gather_pair(fsdp_count, ctx_count, local_pair)
+    attended, exact, log_sum = attend(rank, deal_order, doc_starts, query, pair)
+    (
+        mixed_out,
+        normed_ffn,
+        hidden,
+        grad_gate,
+        grad_up,
+        grad_resid,
+        grad_branch,
+        grad_attended,
+        ffn_gain_part,
+    ) = feed(pack_in, grad_mixed, attended, ffn_gain, out_full, gate_full, up_full, down_full)
+    grad_query, grad_pair = attend_back(
+        rank, deal_order, doc_starts, query, pair, grad_attended, exact, log_sum
+    )
+    grad_pair = scatter_pair(fsdp_count, ctx_count, grad_pair)
+    grad_projected, tokens_grad, attn_gain_part, qk_gain_part = project_back(
+        pack_in,
+        qkv_full,
+        attn_gain,
+        qk_gain,
+        raw,
+        cosines,
+        sines,
+        grad_query,
+        grad_pair,
+        grad_resid,
+    )
     core = ctx_rank % 2
     swap = [(i, i + 1 - 2 * (i % 2)) for i in range(ctx_count)]
 
@@ -931,7 +1200,7 @@
         other = lax.ppermute(core_part(values, 1 - core), "ctx", swap)
         return jnp.concatenate([mine, other], axis=0)
 
-    ffn_rows = both_part(normed_ffn_low)
+    ffn_rows = both_part(normed_ffn)
     parts = [
         transposed_times(left, right).astype(jnp.bfloat16)
         for left, right in (
@@ -939,29 +1208,21 @@
             (ffn_rows, both(grad_gate)),
             (ffn_rows, both(grad_up)),
             (both_part(attended), both(grad_branch)),
-            (both_part(normed_low), both(grad_projected)),
+            (both_part(normed), both(grad_projected)),
         )
     ]
-    gain_sums = pack_rows(
-        [
-            jnp.sum(attn_gain_part, axis=0),
-            jnp.sum(ffn_gain_part, axis=0),
-            jnp.sum(query_gain_part, axis=(0, 1)),
-            jnp.sum(key_gain_part, axis=(0, 1)),
-        ],
-        8,
-    )
+    gain_sums = pack_rows([attn_gain_part, ffn_gain_part, qk_gain_part[:, :HEAD_SIZE]], 8)
     (down_grad, gate_grad, up_grad, out_grad, qkv_grad), gain_sums = reduce_gradients(
         fsdp_count, ctx_count, parts, gain_sums
     )
     gain_sums = gain_sums.reshape(-1)
-    model = model_shard * fsdp_count
-    rank = lax.axis_index("fsdp")
-    attn_gain_grad = lax.dynamic_slice_in_dim(gain_sums, rank * model_shard, model_shard)
-    ffn_gain_grad = lax.dynamic_slice_in_dim(gain_sums, model + rank * model_shard, model_shard)
+    attn_gain_grad = lax.dynamic_slice_in_dim(gain_sums, fsdp_rank * model_shard, model_shard)
+    ffn_gain_grad = lax.dynamic_slice_in_dim(
+        gain_sums, model + fsdp_rank * model_shard, model_shard
+    )
     qk_gain_grad = lax.dynamic_slice_in_dim(
         gain_sums[2 * model : 2 * model + 2 * HEAD_SIZE].reshape(2, HEAD_SIZE),
-        rank * qk_shard,
+        fsdp_rank * qk_shard,
         qk_shard,
         axis=1,
     )
@@ -977,12 +1238,6 @@
         ffn_gain_grad,
         qk_gain_grad,
     )
-
-
-def pack_rows(arrays, multiple):
-    flat = jnp.concatenate([a.astype(jnp.float32).reshape(-1) for a in arrays])
-    size = multiple * 128
-    return jnp.pad(flat, (0, -flat.shape[0] % size)).reshape(-1, 128)
 
 
 def solution(mesh):

time: 590 us -> 407 us (0.69)
  matrix products: 178 us -> 20.5 us
  Pallas kernels: 268 us -> 332 us
  other arithmetic: 65.4 us -> 13.2 us
  local copies, waits for them, and re-layouts: 66.5 us -> 29.4 us
    dot_general x46 -> x0, matrix products: 159 us -> none  [the longest x12 40.4 us: block_scores(): jnp.einsum('qkgd,tkd->kgqt', grouped_heads, key_tile, preferred_element_t...]
    pallas_call x0 -> x5, Pallas kernels: none -> 61.6 us  [the longest x1 17.4 us: feed(): pl.pallas_call(feed_kernel, out_shape=[shape((rows, width), low), shape((...]
    reduce_sum x11 -> x0, other arithmetic: 23.3 us -> none  [the longest x4 20.3 us: stats_step(): jnp.sum(jnp.exp(scores - new_max[..., None]), axis=-1)]
    convert_element_type x5 -> x0, local copies, waits for them, and re-layouts: 11.8 us -> none  [the longest x2 7.2 us: per_device(): pack_in = tokens[0].astype(jnp.float32)]
    unnamed x150 -> x48, local copies, waits for them, and re-layouts: 21.9 us -> 13.7 us
    reshape x5 -> x1, local copies, waits for them, and re-layouts: 6.16 us -> 0.09 us  [per_device(): jnp.swapaxes(qk_gain.reshape(fsdp_count, 2, qk_shard), 0, 1)]
    slice x8 -> x0, local copies, waits for them, and re-layouts: 6.04 us -> none  [the longest x1 2.65 us: per_device(): every_pair[:, :key_value_width]]
    add x13 -> x0, other arithmetic: 6 us -> none  [the longest x3 5.65 us: per_device(): jnp.repeat(deal_order, block_len, total_repeat_length=full_len) * block_len]
  transfers between devices with their start and end apart: 9 -> 9, of which waited for: 0 -> 0; matrix products, arithmetic and copies ran while one was open for 49% -> 8% of each run, Pallas kernels for 23% -> 11%
where the time goes in v2:
time: 407 us; the launch traced here: 400 us
  Pallas kernels  332 us (82%)
  local copies, waits for them, and re-layouts  29.4 us (7%)
  matrix products  20.5 us (5%)
  other arithmetic  13.2 us (3%)
    pallas_call x1, Pallas kernels, reduce_gradients(): pl.pallas_call(functools.partial(reduce_kernel, nf, nc, count), out_shape...  138 us
    pallas_call x1, Pallas kernels, gather_weights(): pl.pallas_call(functools.partial(gather_kernel, nf, nc, count), out_shape...  101 us
    dot_general x5, matrix products, transposed_times(): lax.dot_general(left, right, (((0,), (0,)), ((), ())), preferred_element_...  20.5 us
    pallas_call x1, Pallas kernels, feed(): pl.pallas_call(feed_kernel, out_shape=[shape((rows, width), low), shape((...  17.4 us
    pallas_call x1, Pallas kernels, scatter_pair(): pl.pallas_call(functools.partial(scatter_pair_kernel, nf, nc), out_shape=...  16.7 us
    pallas_call x1, Pallas kernels, attend_back(): pl.pallas_call(attend_back_kernel, out_shape=[jax.ShapeDtypeStruct(query....  16.5 us
    pallas_call x1, Pallas kernels, gather_pair(): pl.pallas_call(functools.partial(gather_pair_kernel, nf, nc), out_shape=j...  15 us
    unnamed x48, local copies, waits for them, and re-layouts  13.7 us
  transfers between devices with their start and end apart: 9, of which 0 were waited for; matrix products, arithmetic and copies ran while one was open for 8% of the time, Pallas kernels for 11%

profile of v2, /device:TPU:1, one launch (start us, length us, event | category | flops | bytes accessed | tf_op | source)
XLA Modules:
  0.0 400.0 jit_solution(15135052545090635206)
XLA Ops:
  0.6 0.7 reshape.190
  1.4 1.3 fusion.31.refs_5_
  2.7 101.5 %gather_weights.1 = (bf16[4,2,2,2,64,1536]{5,4,3,2,1,0:T(8,128)(2,1)}, bf16[4,2,2,2,32,2048]{5,4,3,2,1,0:T(8,128)(2,1)}, bf16[4,2,2,2,64,1024]{5,4,3,2,1,0:T(8,1...) custom-call(bf16[2,2,2,64,1536]{4,3,2,1,0:T(8,128)(2,1)} %bitcast.88, ...), custom_call_target="tpu_custom_call" | custom-call | tf_op jit(solution)/shard_map/gather_weights/pallas_call | solution.py:232
  104.2 0.8 copy.44
  105.0 0.6 copy.41
  105.6 0.1 reshape.196
  105.7 0.1 reshape.197
  105.8 0.6 pad_maximum_fusion.3.qk_gain
  106.4 0.6 maximum_bitcast_fusion.frequency
  107.0 7.7 %project.1 = (bf16[256,2048]{1,0:T(8,128)(2,1)}, f32[256,1536]{1,0:T(8,128)}, bf16[256,1024]{1,0:T(8,128)(2,1)}, bf16[256,512]{1,0:T(8,128)(2,1)}, f32[256,128]{1,0:T(8,128)}, /*index=5*/f32[256,128]{1,0:T(8,128)}) custom-call(s32[1]{0:T(128)} %bitcast.2.rank, s32[16]{0:T(128)} %order.5, s32[1,8]{1,0:T(1,128)} %starts.5, bf16[256,2048]{1,0:T(8,128)(2,1)} %bitcast.75, ...), custom_call_target="tpu_custom_call" | custom-call | tf_op jit(solution)/shard_map/project/pallas_call | solution.py:929
  114.7 15.0 %gather_pair.1 = bf16[2,2,2,256,512]{4,3,2,1,0:T(8,128)(2,1)} custom-call(bf16[256,512]{1,0:T(8,128)(2,1)} %get-tuple-element.49.pair), custom_call_target="tpu_custom_call" | custom-call | tf_op jit(solution)/shard_map/gather_pair/pallas_call | solution.py:295
  129.7 0.6 copy.42
  130.3 10.3 %attend.1 = (bf16[256,1024]{1,0:T(8,128)(2,1)}, f32[256,1024]{1,0:T(8,128)}, f32[2,4,8,512]{3,2,1,0:T(8,128)}) custom-call(s32[1]{0:T(128)} %bitcast.2.rank, s32[16]{0:T(128)} %order.5, s32[1,8]{1,0:T(1,128)} %starts.5, bf16[256,1024]{1,0:T(8,128)(2,1)} %get-tuple-element.48.query, bf16[2048,512]{1,0:T(8,128)(2,1)} %bitcast.73), custom_call_target="tpu_custom_call" | custom-call | tf_op jit(solution)/shard_map/attend/pallas_call | solution.py:748
  140.6 17.4 %feed.1 = (bf16[256,2048]{1,0:T(8,128)(2,1)}, bf16[256,2048]{1,0:T(8,128)(2,1)}, bf16[256,1024]{1,0:T(8,128)(2,1)}, bf16[256,1024]{1,0:T(8,128)(2,1)}, bf16[256,...) custom-call(bf16[256,2048]{1,0:T(8,128)(2,1)} %bitcast.76, ...), custom_call_target="tpu_custom_call" | custom-call | tf_op jit(solution)/shard_map/feed/pallas_call | solution.py:1012
  158.0 0.0 copy-start.7
  158.0 1.9 reshape.210
  160.0 0.8 reshape.219
  160.8 5.5 %constant_dynamic-slice_fusion.2 = (bf16[256,4,1,256]{3,2,1,0:T(2,128)(2,1)}, bf16[256,4,1,256]{3,2,1,0:T(2,128)(2,1)}, bf16[256,4,1,256]{3,2,1,0:T(2,128)(2,1)}, bf16[256,4,1,256]{3,2,1,0:T(2,128)(2,1)S(1)}) fusion(bf16[256,4,2,256]{3,2,1,0:T(2,128)(2,1)S(1)} %reshape.219, s32[]{:T(128)S(6)} %select_n.31, s32[]{:T(128)S(6)} %select_n.32, ...), kind=kLoop, calls=%fused_computation.52 | loop fusion | bytes 4194312 | tf_op jit(solution)/shard_map/jit(dynamic_index_in_dim)/dynamic_slice | solution.py:1196
  166.3 2.3 copy.35
  168.7 0.1 collective-permute-start.2
  168.7 0.5 collective-permute-start.4
  169.2 0.1 collective-permute-start.6
  169.3 16.5 %attend_back.1 = (f32[256,1024]{1,0:T(8,128)}, bf16[2048,512]{1,0:T(8,128)(2,1)}) custom-call(s32[1]{0:T(128)} %bitcast.2.rank, s32[16]{0:T(128)} %order.5, s32[1,8]{1,0:T(1,128)} %starts.5, bf16[256,1024]{1,0:T(8,128)(2,1)} %get-tuple-element.48.query, bf16[2048,512]{1,0:T(8,128)(2,1)} %bitcast.74, bf16[256,1024]{1,0:T(8,128)(2,1)} %get-tuple-element.59.grad, ...), custom_call_target="tpu_custom_call" | custom-call | tf_op jit(solution)/shard_map/attend_back/pallas_call | solution.py:826
  185.8 16.7 %scatter_pair.1.grad_pair = bf16[256,512]{1,0:T(8,128)(2,1)} custom-call(bf16[2,2,2,256,512]{4,3,2,1,0:T(8,128)(2,1)} %bitcast.83), custom_call_target="tpu_custom_call" | custom-call | tf_op jit(solution)/shard_map/scatter_pair/pallas_call | solution.py:375
  202.5 9.7 %project_back.1 = (bf16[256,1536]{1,0:T(8,128)(2,1)}, f32[256,2048]{1,0:T(8,128)}, f32[1,2048]{1,0:T(1,128)}, f32[2,128]{1,0:T(2,128)}) custom-call(bf16[256,2048]{1,0:T(8,128)(2,1)} %bitcast.77, bf16[2048,1536]{1,0:T(8,128)(2,1)} %bitcast.72, f32[1,2048]{1,0:T(1,128)} %bitcast.105, f32[2,128]{1,0:T(2,128)} %pad_maximum_fusion.3.qk_gain, ...), custom_call_target="tpu_custom_call" | custom-call | tf_op jit(solution)/shard_map/project_back/pallas_call | solution.py:1091
  212.1 1.3 collective-permute-start.8
  213.4 0.1 collective-permute-start.1
  213.5 0.4 reshape.215
  213.9 0.5 collective-permute-start.3
  214.4 1.9 constant_dynamic-slice_fusion.4
  216.2 0.1 reshape.225
  216.3 3.5 copy.39
  219.9 2.0 copy.38
  221.8 1.5 copy.37
  223.4 0.5 copy.36
  223.8 0.9 copy.34
  224.8 0.4 reshape.206
  225.2 0.0 collective-permute-done.4
  225.2 0.1 collective-permute-start.7
  225.3 1.1 constant_dynamic-slice_fusion.8
  226.4 0.5 copy.33
  226.9 0.5 copy.32
  227.4 0.6 fusion.24.refs_5_
  228.0 4.0 %convolution_convert_fusion.3 = bf16[1024,1024]{1,0:T(8,128)(2,1)} fusion(bf16[256,1024]{1,0:T(8,128)(2,1)} %collective-permute-done.4, bf16[256,1024]{1,0:T(8,128)(2,1)} %get-tuple-element.69, bf16[256,1024]{0,1:T(8,128)(2,1)} %collective-permute-done.2, bf16[256,1024]{0,1:T(8,128)(2,1)S(1)} %bitcast.95), kind=kOutput, calls=%fused_computation.9 | convolution fusion | flops 1078984704 | bytes 4194304 | tf_op jit(solution)/shard_map/dot_general | solution.py:1107
  232.0 0.0 copy-start.15
  232.0 0.5 collective-permute-start.5
  232.5 3.8 convolution_convert_fusion.4
  236.3 0.0 collective-permute-done.7
  236.3 0.2 collective-permute-start
  236.5 0.0 collective-permute-done.8
  236.5 4.8 %convolution_convert_fusion = bf16[1024,1536]{1,0:T(8,128)(2,1)} fusion(bf16[256,1536]{1,0:T(8,128)(2,1)} %collective-permute-done.8, bf16[256,1536]{1,0:T(8,128)(2,1)S(1)} %copy-done.15, bf16[256,1024]{0,1:T(8,128)(2,1)} %collective-permute-done.7, bf16[256,1024]{0,1:T(8,128)(2,1)S(1)} %bitcast.93), kind=kOutput, calls=%fused_computation | convolution fusion | flops 1617428480 | bytes 5767168 | tf_op jit(solution)/shard_map/dot_general | solution.py:1107
  241.4 3.8 convolution_convert_fusion.1
  245.2 0.0 collective-permute-done
  245.2 4.1 %convolution_convert_fusion.2 = bf16[512,2048]{1,0:T(8,128)(2,1)} fusion(bf16[256,2048]{1,0:T(8,128)(2,1)} %collective-permute-done.1, bf16[256,2048]{1,0:T(8,128)(2,1)} %bitcast.1.cotangent, bf16[256,512]{0,1:T(8,128)(2,1)S(1)} %collective-permute-done, bf16[256,512]{0,1:T(8,128)(2,1)S(1)} %bitcast.100), kind=kOutput, calls=%fused_computation.2 | convolution fusion | flops 1080033280 | bytes 4718592 | tf_op jit(solution)/shard_map/dot_general | solution.py:1107
  249.3 137.7 %reduce_gradients.1 = (bf16[2,2,2,32,2048]{4,3,2,1,0:T(8,128)(2,1)}, bf16[2,2,2,64,1024]{4,3,2,1,0:T(8,128)(2,1)}, bf16[2,2,2,64,1024]{4,3,2,1,0:T(8,128)(2,1)},...) custom-call(bf16[4,2,2,32,2048]{4,3,2,1,0:T(8,128)(2,1)} %bitcast.87, ...), custom_call_target="tpu_custom_call" | custom-call | tf_op jit(solution)/shard_map/reduce_gradients/pallas_call | solution.py:590
  387.0 3.6 bitcast_convert_fusion
  390.6 1.6 bitcast_convert_fusion.1
  392.2 1.6 bitcast_convert_fusion.2
  393.9 1.6 bitcast_convert_fusion.3
  395.5 1.6 bitcast_convert_fusion.4
  397.1 0.7 slice_reduce_fusion
  397.8 0.1 reshape.228
  397.9 0.6 constant_dynamic-slice_fusion
  398.6 1.3 fusion.37
  (43 shorter events, 0.1 us)
Async XLA Ops:
  158.0 1.9 copy-start.7
  168.7 45.2 %collective-permute-start.2 = (bf16[256,1024]{0,1:T(8,128)(2,1)S(1)}, bf16[256,1024]{0,1:T(8,128)(2,1)}, u32[]{:S(2)}, u32[]{:S(2)}) collective-permute-start(bf16[256,1024]{0,1:T(8,128)(2,1)S(1)} %bitcast.97), channel_id=1, source_target_pairs={{0,4},{4,0},{8,12},{12,8},{16,20},{20,16},{24,28},{28,24},{1,5},{5... | collective-permute-start | bytes 1572872 | tf_op jit(solution)/shard_map/ppermute | solution.py:1200
  168.7 56.4 %collective-permute-start.4 = (bf16[256,1024]{1,0:T(8,128)(2,1)}, bf16[256,1024]{1,0:T(8,128)(2,1)}, u32[]{:S(2)}, u32[]{:S(2)}) collective-permute-start(bf16[256,1024]{1,0:T(8,128)(2,1)} %get-tuple-element.69), channel_id=1, source_target_pairs={{0,4},{4,0},{8,12},{12,8},{16,20},{20,16},{24,28},{28,24},{1,5},{5... | collective-permute-start | bytes 1572872 | tf_op jit(solution)/shard_map/ppermute | solution.py:1192
  169.2 72.1 %collective-permute-start.6 = (bf16[256,2048]{1,0:T(8,128)(2,1)}, bf16[256,2048]{1,0:T(8,128)(2,1)}, u32[]{:S(2)}, u32[]{:S(2)}) collective-permute-start(bf16[256,2048]{1,0:T(8,128)(2,1)} %get-tuple-element.70), channel_id=1, source_target_pairs={{0,4},{4,0},{8,12},{12,8},{16,20},{20,16},{24,28},{28,24},{1,5},{5... | collective-permute-start | bytes 3145736 | tf_op jit(solution)/shard_map/ppermute | solution.py:1192
  202.5 11.0 %copy-start.1 = (bf16[256,1024]{1,0:T(8,128)(2,1)S(1)}, bf16[256,1024]{1,0:T(8,128)(2,1)}, u32[]{:S(2)}) copy-start(bf16[256,1024]{1,0:T(8,128)(2,1)} %get-tuple-element.50.attended) | copy-start | bytes 1572868
  212.1 4.1 %copy-start.17 = (f32[2,128]{1,0:T(2,128)S(1)}, f32[2,128]{1,0:T(2,128)}, u32[]{:S(2)}) copy-start(f32[2,128]{1,0:T(2,128)} %get-tuple-element.75) | copy-start | bytes 3076
  212.1 24.3 %collective-permute-start.8 = (bf16[256,1536]{1,0:T(8,128)(2,1)}, bf16[256,1536]{1,0:T(8,128)(2,1)}, u32[]{:S(2)}, u32[]{:S(2)}) collective-permute-start(bf16[256,1536]{1,0:T(8,128)(2,1)} %get-tuple-element.72), channel_id=1, source_target_pairs={{0,4},{4,0},{8,12},{12,8},{16,20},{20,16},{24,28},{28,24},{1,5},{5... | collective-permute-start | bytes 2359304 | tf_op jit(solution)/shard_map/ppermute | solution.py:1192
  213.4 31.8 %collective-permute-start.1 = (bf16[256,2048]{1,0:T(8,128)(2,1)}, bf16[256,2048]{1,0:T(8,128)(2,1)}, u32[]{:S(2)}, u32[]{:S(2)}) collective-permute-start(bf16[256,2048]{1,0:T(8,128)(2,1)} %bitcast.1.cotangent), channel_id=1, source_target_pairs={{0,4},{4,0},{8,12},{12,8},{16,20},{20,16},{24,28},{28,24},{1,5},{5... | collective-permute-start | bytes 3145736 | tf_op jit(solution)/shard_map/ppermute | solution.py:1192
  213.8 6.0 %copy-start = (bf16[256,4,1,256]{3,2,1,0:T(2,128)(2,1)S(1)}, bf16[256,4,1,256]{3,2,1,0:T(2,128)(2,1)}, u32[]{:S(2)}) copy-start(bf16[256,4,1,256]{3,2,1,0:T(2,128)(2,1)} %get-tuple-element.82) | copy-start | bytes 1572868
  213.9 18.2 %collective-permute-start.3 = (bf16[256,1024]{1,0:T(8,128)(2,1)}, bf16[256,1024]{1,0:T(8,128)(2,1)}, u32[]{:S(2)}, u32[]{:S(2)}) collective-permute-start(bf16[256,1024]{1,0:T(8,128)(2,1)} %get-tuple-element.68), channel_id=1, source_target_pairs={{0,4},{4,0},{8,12},{12,8},{16,20},{20,16},{24,28},{28,24},{1,5},{5... | collective-permute-start | bytes 1572872 | tf_op jit(solution)/shard_map/ppermute | solution.py:1192
  216.2 5.6 %copy-start.2 = (bf16[256,4,1,128]{3,2,1,0:T(2,128)(2,1)S(1)}, bf16[256,4,1,128]{3,2,1,0:T(2,128)(2,1)}, u32[]{:S(2)}) copy-start(bf16[256,4,1,128]{3,2,1,0:T(2,128)(2,1)} %get-tuple-element.87) | copy-start | bytes 786436
  221.8 2.9 copy-start.10
  221.8 3.3 copy-start.9
  225.1 2.2 copy-start.12
  225.1 2.2 copy-start.13
  225.2 11.1 %collective-permute-start.7 = (bf16[256,1024]{0,1:T(8,128)(2,1)S(1)}, bf16[256,1024]{0,1:T(8,128)(2,1)}, u32[]{:S(2)}, u32[]{:S(2)}) collective-permute-start(bf16[256,1024]{0,1:T(8,128)(2,1)S(1)} %bitcast.94), channel_id=1, source_target_pairs={{0,4},{4,0},{8,12},{12,8},{16,20},{20,16},{24,28},{28,24},{1,5},{5... | collective-permute-start | bytes 1572872 | tf_op jit(solution)/shard_map/ppermute | solution.py:1200
  228.0 4.0 %copy-start.11 = (bf16[256,4,1,128]{0,3,1,2:T(8,128)(2,1)S(1)}, bf16[256,4,1,128]{0,3,1,2:T(8,128)(2,1)}, u32[]{:S(2)}) copy-start(bf16[256,4,1,128]{0,3,1,2:T(8,128)(2,1)} %copy.37) | copy-start | bytes 786436
  228.0 4.5 %copy-start.16 = (bf16[256,1024]{1,0:T(8,128)(2,1)S(1)}, bf16[256,1024]{1,0:T(8,128)(2,1)}, u32[]{:S(2)}) copy-start(bf16[256,1024]{1,0:T(8,128)(2,1)} %get-tuple-element.68) | copy-start | bytes 1572868
  232.0 4.5 %copy-start.8 = (bf16[256,4,1,256]{0,3,1,2:T(8,128)(2,1)S(1)}, bf16[256,4,1,256]{0,3,1,2:T(8,128)(2,1)}, u32[]{:S(2)}) copy-start(bf16[256,4,1,256]{0,3,1,2:T(8,128)(2,1)} %copy.38) | copy-start | bytes 1572868
  232.0 4.5 %copy-start.15 = (bf16[256,1536]{1,0:T(8,128)(2,1)S(1)}, bf16[256,1536]{1,0:T(8,128)(2,1)}, u32[]{:S(2)}) copy-start(bf16[256,1536]{1,0:T(8,128)(2,1)} %get-tuple-element.72) | copy-start | bytes 2359300
  232.0 9.3 %collective-permute-start.5 = (bf16[256,512]{0,1:T(8,128)(2,1)S(1)}, bf16[256,512]{0,1:T(8,128)(2,1)S(1)}, u32[]{:S(2)}, u32[]{:S(2)}) collective-permute-start(bf16[256,512]{0,1:T(8,128)(2,1)S(1)} %bitcast.99), channel_id=1, source_target_pairs={{0,4},{4,0},{8,12},{12,8},{16,20},{20,16},{24,28},{28,24},{1,5},{5... | collective-permute-start | bytes 786440 | tf_op jit(solution)/shard_map/ppermute | solution.py:1200
  236.3 8.8 %collective-permute-start = (bf16[256,512]{0,1:T(8,128)(2,1)S(1)}, bf16[256,512]{0,1:T(8,128)(2,1)S(1)}, u32[]{:S(2)}, u32[]{:S(2)}) collective-permute-start(bf16[256,512]{0,1:T(8,128)(2,1)S(1)} %bitcast.101), channel_id=1, source_target_pairs={{0,4},{4,0},{8,12},{12,8},{16,20},{20,16},{24,28},{28,24},{1,5},{5... | collective-permute-start | bytes 786440 | tf_op jit(solution)/shard_map/ppermute | solution.py:1200
  236.5 4.9 %copy-start.14 = (bf16[256,2048]{1,0:T(8,128)(2,1)S(1)}, bf16[256,2048]{1,0:T(8,128)(2,1)}, u32[]{:S(2)}) copy-start(bf16[256,2048]{1,0:T(8,128)(2,1)} %get-tuple-element.70) | copy-start | bytes 3145732
  387.0 3.6 copy-start.6
  390.6 1.6 copy-start.5
  392.2 1.6 copy-start.4
  393.9 1.6 copy-start.3
